TPU v7x, 32 devices: a whole 2x2x4 slice. The times are simulated.
32 devices in a mesh: dp: 8 (over y, x, core), fsdp: 4 (over z).
Axes of the slice: x: 2, y: 2, z: 4, core: 2. Of those that a mesh axis runs over, the one named last changes fastest.
Arguments:
- glu_frames: bfloat16 [8192, 1536], P(('dp', 'fsdp')), may hold values from -6 to 6
- residual_frames: bfloat16 [8192, 1536], P(('dp', 'fsdp')), may hold values from -6 to 6
- send_rows: int32 [8, 4, 8, 32], P('dp', 'fsdp'), may hold values from 0 to 255, as said below
- recv_slot: int32 [8, 4, 128], P('dp', 'fsdp'), may hold values from 0 to 255, as said below
- segment_ids: int32 [8, 4, 128], P('dp', 'fsdp'), may hold values from 0 to 15, never falling along the last dimension, each value on 1 to 64 neighbouring positions
- code_targets: int32 [8, 512], P('dp'), may hold values from 0 to 8191
- conv_kernel: float32 [31, 1536], replicated, may hold values from -1 to 1
- norm_gain: float32 [1536], replicated, may hold values from 0.5 to 1.5
- point_weight: bfloat16 [1536, 1536], P('fsdp'), may hold values from -0.15625 to 0.15625
- code_head: bfloat16 [1536, 8192], P(None, 'fsdp')
Outputs:
- loss: float32 [], replicated
- grad_head: float32 [1536, 8192], P('dp', 'fsdp')
- grad_point: float32 [1536, 1536], P('fsdp', 'dp')
- grad_kernel: float32 [31, 1536], replicated
- grad_gain: float32 [1536], replicated
- grad_residual: bfloat16 [4096, 1536], P(('dp', 'fsdp'))
- grad_glu: bfloat16 [4096, 1536], P(('dp', 'fsdp'))
Inputs may be any that keep to these rules, and one draw needn't show every extreme that they name: send_rows[i, f, o] lists 32 local slots of loading device (i, f) for owner (o, f). Each loading device fills whole buckets for between 2 and 8 owners, at most one bucket per owner, with distinct slots; its entries for other owners are never read. recv_slot[o, f, r] = i * 32 + c names position c of the bucket from loading device (i, f). Each owner reads 4 full buckets of 32 frames, from distinct loading devices, each whole and in order.
All inputs are finite; a program needn't handle non-finite values.
Results may differ from a plain program's by a relative error of at most 0.012.
The roundings to bfloat16 on the way count: a program that leaves them out, or rounds other values in their place, can miss the bound.
Values may be sent and summed in bfloat16 or wider, within the bound.
No kernel may reach another device: no remote copies, remote signals or barrier semaphores. Data moves between devices by JAX's collectives and lax.ppermute only.
A program may use at most 128 MiB of HBM per device.

v0:
```python
import functools

import jax
import jax.numpy as jnp
from jax import lax
from jax.experimental import pallas as pl
from jax.experimental.pallas import tpu as pltpu
from jax.sharding import PartitionSpec as P

F32 = jnp.float32
BF16 = jnp.bfloat16


def flip_dp(value, mask):
    count = lax.axis_size("dp")
    return lax.ppermute(value, "dp", [(i, i ^ mask) for i in range(count)])


def flip_fsdp(value, mask):
    count = lax.axis_size("fsdp")
    return lax.ppermute(value, "fsdp", [(i, i ^ mask) for i in range(count)])


def shift_fsdp(value, step):
    count = lax.axis_size("fsdp")
    return lax.ppermute(value, "fsdp", [(i, (i + step) % count) for i in range(count)])


def pick(array, index, axis=0):
    return lax.dynamic_index_in_dim(array, index, axis, keepdims=False)


def ordered(bit, own, other, axis):
    return jnp.where(
        bit == 0, jnp.stack([own, other], axis), jnp.stack([other, own], axis)
    )


def tree_sum(values):
    while len(values) > 1:
        values = [values[i] + values[i + 1] for i in range(0, len(values), 2)]
    return values[0]


def after(value, *others):
    return lax.optimization_barrier((value, *others))[0]


def gather_point(point_weight, d, activation):
    count = lax.axis_size("fsdp")
    rows, width = point_weight.shape
    core, bit1, bit2 = d & 1, (d >> 1) & 1, (d >> 2) & 1
    parts = point_weight.reshape(2, 2, 2, rows // 8, width)
    piece1 = pick(pick(parts[0], bit1), core)
    piece2 = pick(pick(parts[1], bit2), core)
    piece = jnp.stack([piece1, piece2])
    got = jnp.stack([shift_fsdp(piece, step) for step in range(1, count)], 1)
    across = [flip_dp(got[0], 2), flip_dp(got[1], 4)]
    far = [flip_dp(got, 1)] + [flip_dp(after(piece, activation), 1) for piece in across]
    return [got] + across + far


def branch_kernel(
    place, weight, act, residual, got, got1, got2, far, far1, far2, kept, out, panel, sems, keep
):
    count = panel.shape[0]
    d, f = place[0], place[1]
    core, bits = d & 1, ((d >> 1) & 1, (d >> 2) & 1)
    copies = [(weight, panel.at[f])]
    for step in range(1, count):
        shard = panel.at[lax.rem(f + count - step, count)]
        for mine, others, side in (
            (got, (got1, got2), core),
            (far, (far1, far2), 1 - core),
        ):
            for half in range(2):
                copies.append((mine.at[half, step - 1], shard.at[half, bits[half], side]))
                copies.append((others[half].at[step - 1], shard.at[half, 1 - bits[half], side]))
    copies = [
        pltpu.make_async_copy(source, target, sems.at[i])
        for i, (source, target) in enumerate(copies)
    ]
    for copy in copies:
        copy.start()
    for copy in copies:
        copy.wait()
    keeping = pltpu.make_async_copy(panel, kept, keep)
    keeping.start()
    rows, width = act.shape
    tile = 512
    whole = panel.reshape(act.shape[1], width)

    @pl.loop(0, width // tile)
    def _(step):
        lanes = pl.ds(pl.multiple_of(step * tile, tile), tile)
        total = jnp.dot(act[...], whole[:, lanes], preferred_element_type=F32)
        out[:, lanes] = (residual[:, lanes].astype(F32) + total).astype(BF16)

    keeping.wait()


def branch(point_weight, activation, residual_owned, pieces, d, f):
    count = lax.axis_size("fsdp")
    rows, width = point_weight.shape
    vmem = pl.BlockSpec(memory_space=pltpu.VMEM)
    panel, out = pl.pallas_call(
        branch_kernel,
        out_shape=(
            jax.ShapeDtypeStruct((count, 2, 2, 2, rows // 8, width), BF16),
            jax.ShapeDtypeStruct(activation.shape, BF16),
        ),
        in_specs=[pl.BlockSpec(memory_space=pltpu.SMEM), pl.BlockSpec(memory_space=pltpu.HBM)]
        + [vmem] * 2
        + [pl.BlockSpec(memory_space=pl.ANY)] * 6,
        out_specs=(pl.BlockSpec(memory_space=pltpu.HBM), vmem),
        scratch_shapes=[
            pltpu.VMEM((count, 2, 2, 2, rows // 8, width), BF16),
            pltpu.SemaphoreType.DMA((1 + 8 * (count - 1),)),
            pltpu.SemaphoreType.DMA,
        ],
        compiler_params=pltpu.CompilerParams(vmem_limit_bytes=60 << 20),
        name="branch",
    )(
        jnp.stack([d, f]),
        point_weight.reshape(2, 2, 2, rows // 8, width),
        activation,
        residual_owned,
        *pieces,
    )
    return panel.reshape(count * rows, width), out


EDGE = 16


def forward_kernel(
    sent, slots, masks, kernel, gain, glu, residual, standard, inv_std, act, padded, received, sem
):
    copy = pltpu.make_async_copy(sent, received, sem)
    copy.start()
    rows, width = standard.shape
    tap_count = masks.shape[0]
    half_taps = tap_count // 2
    loaders, both, _ = received.shape
    capacity = both // 2
    places = lax.broadcasted_iota(jnp.int32, (rows, loaders * capacity), 1)
    chosen = (slots[...] == places).astype(BF16)
    tile = 512
    tiles = [slice(i, i + tile) for i in range(0, width, tile)]
    for edge in (0, EDGE + rows):
        padded[pl.ds(edge, EDGE), :] = jnp.zeros((EDGE, width), F32)
    copy.wait()
    for lanes in tiles:
        for start, target in ((0, glu), (capacity, residual)):
            frames = received[:, start : start + capacity, lanes]
            frames = frames.reshape(loaders * capacity, tile)
            owned = jnp.dot(chosen, frames, preferred_element_type=F32)
            target[:, lanes] = owned.astype(BF16)
            if start == 0:
                padded[pl.ds(EDGE, rows), lanes] = owned

    @pl.loop(0, width // 128)
    def _(step):
        lanes = pl.ds(pl.multiple_of(step * 128, 128), 128)
        total = jnp.zeros((rows, 128), F32)
        for tap in range(tap_count):
            moved = padded[pl.ds(EDGE + tap - half_taps, rows), lanes]
            total = total + kernel[pl.ds(tap, 1), lanes] * (masks[tap] * moved)
        standard[:, lanes] = total

    mean = sum(jnp.sum(standard[:, lanes], axis=1, keepdims=True) for lanes in tiles) / width
    square = jnp.zeros((rows, 1), F32)
    for lanes in tiles:
        centred = standard[:, lanes] - mean
        square = square + jnp.sum(centred * centred, axis=1, keepdims=True)
    scale = lax.rsqrt(square / width + 1e-05)
    inv_std[...] = scale
    for lanes in tiles:
        unit = (standard[:, lanes] - mean) * scale
        standard[:, lanes] = unit
        normed = unit * gain[:, lanes]
        act[:, lanes] = (normed * jax.nn.sigmoid(normed)).astype(BF16)


def forward(received, slot_list, masks, kernel, gain):
    rows, width = slot_list.shape[0], received.shape[2]
    vmem = pl.BlockSpec(memory_space=pltpu.VMEM)
    half = jax.ShapeDtypeStruct((rows, width), BF16)
    return pl.pallas_call(
        forward_kernel,
        out_shape=(
            half,
            half,
            jax.ShapeDtypeStruct((rows, width), F32),
            jax.ShapeDtypeStruct((rows, 1), F32),
            half,
        ),
        in_specs=[pl.BlockSpec(memory_space=pltpu.HBM)] + [vmem] * 4,
        out_specs=(vmem,) * 5,
        scratch_shapes=[
            pltpu.VMEM((rows + 2 * EDGE, width), F32),
            pltpu.VMEM(received.shape, BF16),
            pltpu.SemaphoreType.DMA,
        ],
        compiler_params=pltpu.CompilerParams(vmem_limit_bytes=60 << 20),
        cost_estimate=pl.CostEstimate(
            flops=1_000_000_000, bytes_accessed=6_000_000, transcendentals=200_000
        ),
        name="forward",
    )(received, slot_list[:, None], masks, kernel, gain[None, :])


def code_kernel(count, index, norms, targets, *refs):
    logits, head = refs[:count], refs[count]
    grads, outs = refs[count + 1 : 2 * count + 1], refs[2 * count + 1 : 3 * count + 1]
    norm, target, total, held, sems = refs[3 * count + 1 :]
    rows, codes = logits[0].shape
    parts, _, tile = held.shape
    copies = [
        pltpu.make_async_copy(head.at[:, pl.ds(i * tile, tile)], held.at[i], sems.at[i])
        for i in range(parts)
    ]
    for copy in copies:
        copy.start()
    for i in range(count):
        for table, column in ((norms, norm), (targets, target)):
            line = table[pl.ds(index[i], 1), :]
            column[i] = jnp.broadcast_to(line, (rows, rows)).T
    for part in range(parts):
        lanes = slice(part * tile, (part + 1) * tile)
        columns = lax.broadcasted_iota(jnp.int32, (rows, tile), 1) + part * tile
        values = []
        for i in range(count):
            hits = (columns == target[i][:, :1].astype(jnp.int32)).astype(F32)
            value = (jnp.exp(logits[i][:, lanes] - norm[i][:, :1]) - hits).astype(BF16)
            grads[i][:, lanes] = value
            values.append(value)
        value = jnp.concatenate(values) if count > 1 else values[0]
        copies[part].wait()
        product = lax.dot_general(
            value, held[part], (((1,), (1,)), ((), ())), preferred_element_type=F32
        )
        if part:
            product = total[...] + product
        if part < parts - 1:
            total[...] = product
        else:
            for i in range(count):
                outs[i][...] = product[i * rows : (i + 1) * rows].astype(outs[i].dtype)


def code_grad(logits, index, norms, targets, head, dtype):
    count = len(logits)
    rows, codes = logits[0].shape
    width, tile = head.shape[0], 512
    vmem = pl.BlockSpec(memory_space=pltpu.VMEM)
    made = pl.pallas_call(
        functools.partial(code_kernel, count),
        out_shape=[jax.ShapeDtypeStruct((rows, codes), BF16)] * count
        + [jax.ShapeDtypeStruct((rows, width), dtype)] * count,
        in_specs=[pl.BlockSpec(memory_space=pltpu.SMEM)]
        + [vmem] * (count + 2)
        + [pl.BlockSpec(memory_space=pltpu.HBM)],
        out_specs=[vmem] * (2 * count),
        scratch_shapes=[
            pltpu.VMEM((count, rows, rows), F32),
            pltpu.VMEM((count, rows, rows), F32),
            pltpu.VMEM((count * rows, width), F32),
            pltpu.VMEM((codes // tile, width, tile), BF16),
            pltpu.SemaphoreType.DMA((codes // tile,)),
        ],
        compiler_params=pltpu.CompilerParams(vmem_limit_bytes=(10 + 4 * count) << 20),
        cost_estimate=pl.CostEstimate(
            flops=800_000_000 * count, bytes_accessed=8_000_000, transcendentals=200_000 * count
        ),
        name="code",
    )(index, norms, targets.astype(F32), *logits, head)
    return made[:count], made[count:]


def head_kernel(count, place, *refs):
    rows, grads, mine, sent = refs[:count], refs[count : 2 * count], refs[-2], refs[-1]
    core = place[0]
    pairs, height, codes = mine.shape
    tile = min(512, codes)
    for pair in range(pairs):
        side = slice(2 * pair * height, (2 * pair + 2) * height)
        turned = jnp.concatenate([block[:, side] for block in rows]).T
        for step in range(codes // tile):
            lanes = slice(step * tile, (step + 1) * tile)
            product = jnp.dot(
                turned,
                jnp.concatenate([grad[:, lanes] for grad in grads]),
                preferred_element_type=F32,
            ).astype(BF16)

            @pl.when(core == 0)
            def _():
                mine[pair, :, lanes] = product[:height]
                sent[pair, :, lanes] = product[height:]

            @pl.when(core != 0)
            def _():
                mine[pair, :, lanes] = product[height:]
                sent[pair, :, lanes] = product[:height]


def head_grad(rows, grads, core):
    n_dp = lax.axis_size("dp")
    count = len(rows)
    half = jax.ShapeDtypeStruct((n_dp // 2, rows[0].shape[1] // n_dp, grads[0].shape[1]), BF16)
    vmem = pl.BlockSpec(memory_space=pltpu.VMEM)
    return pl.pallas_call(
        functools.partial(head_kernel, count),
        out_shape=(half, half),
        in_specs=[pl.BlockSpec(memory_space=pltpu.SMEM)] + [vmem] * (2 * count),
        out_specs=(vmem, vmem),
        compiler_params=pltpu.CompilerParams(vmem_limit_bytes=20 << 20),
        cost_estimate=pl.CostEstimate(flops=1000, bytes_accessed=1000, transcendentals=0),
        name="head",
    )(core[None], *rows, *grads)


def point_kernel(count, place, cols, *refs):
    given = refs[:count]
    own, out, acts, parts, sems = refs[count:]
    d, f = place[0], place[1]
    copies = [pltpu.make_async_copy(given[i], acts.at[i], sems.at[i]) for i in range(count)]
    for copy in copies:
        copy.start()
    for copy in copies:
        copy.wait()
    blocks, _, width = out.shape
    for block in range(blocks):
        lanes = slice(block * width, (block + 1) * width)
        total = jnp.zeros(out.shape[1:], F32)
        for mask in range(count):
            total = total + jnp.dot(
                cols[d ^ mask], acts[mask, :, lanes], preferred_element_type=F32
            )
        out[f ^ block] = total.astype(BF16)
        parts[block] = total
    own[...] = parts[f]


def point_part(cols, acts, d, f):
    n_fsdp = lax.axis_size("fsdp")
    width = acts[0].shape[1] // n_fsdp
    vmem = pl.BlockSpec(memory_space=pltpu.VMEM)
    return pl.pallas_call(
        functools.partial(point_kernel, len(acts)),
        out_shape=(
            jax.ShapeDtypeStruct((cols.shape[1], width), F32),
            jax.ShapeDtypeStruct((n_fsdp, cols.shape[1], width), BF16),
        ),
        in_specs=[pl.BlockSpec(memory_space=pltpu.SMEM), vmem]
        + [pl.BlockSpec(memory_space=pltpu.HBM)] * len(acts),
        out_specs=(vmem, vmem),
        scratch_shapes=[
            pltpu.VMEM((len(acts), *acts[0].shape), BF16),
            pltpu.VMEM((n_fsdp, cols.shape[1], width), F32),
            pltpu.SemaphoreType.DMA((len(acts),)),
        ],
        compiler_params=pltpu.CompilerParams(vmem_limit_bytes=60 << 20),
        cost_estimate=pl.CostEstimate(flops=1000, bytes_accessed=1000, transcendentals=0),
        name="point",
    )(jnp.stack([d, f]), cols, *acts)


def gather_rows(own, f):
    count = lax.axis_size("fsdp")
    if count != 4:
        return [(0, own)] + [(count - step, shift_fsdp(own, step)) for step in range(1, count)]
    before = shift_fsdp(own, 1)
    after = shift_fsdp(own, -1)
    source = jnp.where(f == 2, before, jnp.where(f == 1, after, own))
    across = lax.ppermute(source, "fsdp", [(0, 2), (3, 1), (2, 3), (1, 0)])
    return [(0, own), (3, before), (1, after), (2, across)]


def scatter_rows(code_part, gathered, d, f):
    count = lax.axis_size("fsdp")

    places = [distance for distance, _ in gathered]

    def head_halves(grads):
        return head_grad([block for _, block in gathered], [grads[p] for p in places], d & 1)

    if count != 4:
        grads, outs = code_part(places, F32)
        grads, outs = dict(zip(places, grads)), dict(zip(places, outs))
        got = [shift_fsdp(outs[step].astype(BF16), step).astype(F32) for step in range(1, count)]
        return sum(got, outs[0]), join_cores(*head_halves(grads), d)
    grads = {}
    (grads[2],), (block,) = code_part([2], BF16)
    across = lax.ppermute(block, "fsdp", [(2, 0), (1, 3), (3, 2), (0, 1)])
    (grads[1], grads[3], grads[0]), (ahead, behind, own) = code_part([1, 3, 0], F32)
    across = after(across, own).astype(F32)
    ahead = (ahead + jnp.where(f == 1, across, 0.0)).astype(BF16)
    behind = (behind + jnp.where(f == 2, across, 0.0)).astype(BF16)
    got1 = shift_fsdp(ahead, 1)
    got2 = shift_fsdp(behind, -1)
    direct = jnp.where((f == 0) | (f == 3), across, 0.0)
    mine, sent = head_halves({place: after(grads[place], ahead, behind) for place in places})
    sides = join_cores(mine, sent, d)
    got1 = after(got1, *[keep for keep, _, _ in sides])
    return own + direct + got1.astype(F32) + got2.astype(F32), sides


def fold_kernel(cut, place, *refs):
    ins, outs, held, sems = refs[:4], refs[4:8], refs[8:12], refs[12]
    copies = []
    for i, (source, target) in enumerate(zip(ins, held)):
        if cut:
            width = target.shape[-1]
            source = source.at[:, :, :, :, pl.ds(i // 2 * width, width)]
        copies.append(pltpu.make_async_copy(source, target, sems.at[i]))
        copies[-1].start()
    for side in range(2):
        own, other = held[2 * side], held[2 * side + 1]
        copies[2 * side].wait()
        copies[2 * side + 1].wait()
        keep, send = outs[2 * side], outs[2 * side + 1]
        before, _, behind = own.shape[:3]
        for first in range(before):
            for last in range(behind):
                for target, half in ((keep, place[side]), (send, 1 - place[side])):
                    total = own[first, half, last].astype(F32) + other[first, half, last].astype(F32)
                    target[first, last] = total.astype(target.dtype)


def fold(sides, d, cut=False):
    ins, outs, held, left_over = [], [], [], []
    for own, other, left, bit in sides:
        place = left.index(bit)
        rows, width = own.shape[-2:]
        part = width // 2 if cut else width
        before, behind = 2**place, 2 ** (len(left) - 1 - place)
        ins += [value.reshape(before, 2, behind, rows, width) for value in (own, other)]
        held += [pltpu.VMEM((before, 2, behind, rows, part), BF16)] * 2
        outs += [jax.ShapeDtypeStruct((before, behind, rows, part), BF16)] * 2
        left_over.append([b for b in left if b != bit])
    vmem = pl.BlockSpec(memory_space=pltpu.VMEM)
    made = pl.pallas_call(
        functools.partial(fold_kernel, cut),
        out_shape=outs,
        in_specs=[pl.BlockSpec(memory_space=pltpu.SMEM)] + [pl.BlockSpec(memory_space=pl.ANY)] * 4,
        out_specs=[vmem] * 4,
        scratch_shapes=held + [pltpu.SemaphoreType.DMA((4,))],
        compiler_params=pltpu.CompilerParams(vmem_limit_bytes=16 << 20),
        cost_estimate=pl.CostEstimate(flops=1000, bytes_accessed=1000, transcendentals=0),
        name="fold",
    )(jnp.stack([(d >> side[3]) & 1 for side in sides]), *ins)
    return [(made[2 * i], made[2 * i + 1], left_over[i]) for i in range(2)]


def last_kernel(*refs):
    out = refs[4]
    width = refs[0].shape[-1]
    for side in range(2):
        total = refs[2 * side][...].astype(F32) + refs[2 * side + 1][...].astype(F32)
        out[:, side * width : (side + 1) * width] = total


def last_fold(parts):
    rows, width = parts[0].shape[-2:]
    vmem = pl.BlockSpec(memory_space=pltpu.VMEM)
    return pl.pallas_call(
        last_kernel,
        out_shape=jax.ShapeDtypeStruct((rows, 2 * width), F32),
        in_specs=[vmem] * 4,
        out_specs=vmem,
        compiler_params=pltpu.CompilerParams(vmem_limit_bytes=12 << 20),
        cost_estimate=pl.CostEstimate(flops=1000, bytes_accessed=1000, transcendentals=0),
        name="last",
    )(*[part.reshape(rows, width) for part in parts])


def halve_bits(step):
    bits = lax.axis_size("dp").bit_length() - 1
    return [list(range(1, bits))[step], list(range(bits - 1, 0, -1))[step]]


def join_cores(mine, sent, d):
    left = list(range(lax.axis_size("dp").bit_length() - 2, 0, -1))
    got = flip_dp(sent, 1)
    sides = [(mine, got, left, bit) for bit in halve_bits(0)]
    return send_on(fold(sides, d, True), 0)


def send_on(folded, step):
    return [
        (keep, flip_dp(send, 1 << bit), left)
        for (keep, send, left), bit in zip(folded, halve_bits(step))
    ]


def middle_folds(sides, d):
    bits = lax.axis_size("dp").bit_length() - 1
    for step in range(1, bits - 1):
        ready = [(*side, bit) for side, bit in zip(sides, halve_bits(step))]
        sides = send_on(fold(ready, d), step)
    return sides


def taps_kernel(
    grad, panel, standard, inv_std, gain, glu, masks, loss, packet, conv_grad, scaled, padded, *held
):
    rows, width = standard.shape
    tap_count = masks.shape[0]
    half_taps = tap_count // 2
    tile = 512
    panel_held, standard_held, glu_held, masks_held, sems = held
    copies = [
        pltpu.make_async_copy(source, target, sems.at[i])
        for i, (source, target) in enumerate(
            [(standard, standard_held)]
            + [
                (panel.at[pl.ds(i * tile, tile)], panel_held.at[pl.ds(i * tile, tile)])
                for i in range(width // tile)
            ]
            + [(glu, glu_held), (masks, masks_held)]
        )
    ]
    for copy in copies:
        copy.start()
    panel, standard, glu, masks = panel_held, standard_held, glu_held, masks_held
    copies[0].wait()
    parts = packet.shape[2] // 128
    rest = packet.shape[1] - tap_count - 1
    packet[:, pl.ds(tap_count + 1, rest), :] = jnp.full((2, rest, packet.shape[2]), loss[0, 0])
    sums = jnp.zeros((rows, 1), F32)
    dots = jnp.zeros((rows, 1), F32)
    for lanes in [slice(i, i + tile) for i in range(0, width, tile)]:
        copies[1 + lanes.start // tile].wait()
        act_grad = lax.dot_general(
            grad[...], panel[lanes, :], (((1,), (1,)), ((), ())), preferred_element_type=F32
        )
        scale = gain[:, lanes]
        unit = standard[:, lanes]
        normed = unit * scale
        sig = jax.nn.sigmoid(normed)
        normed_grad = act_grad * sig * (1.0 + normed * (1.0 - sig))
        gain_grad = jnp.sum(normed_grad * unit, axis=0, keepdims=True)
        for first in range(0, tile, 128):
            half, place = divmod(lanes.start + first, packet.shape[2])
            packet[half, pl.ds(tap_count, 1), place : place + 128] = gain_grad[
                :, first : first + 128
            ]
        part = normed_grad * scale
        scaled[:, lanes] = part
        sums = sums + jnp.sum(part, axis=1, keepdims=True)
        dots = dots + jnp.sum(part * unit, axis=1, keepdims=True)
    for copy in copies[-2:]:
        copy.wait()
    sums, dots, scale = sums / width, dots / width, inv_std[...]
    for edge in (0, EDGE + rows):
        conv_grad[pl.ds(edge, EDGE), :] = jnp.zeros((EDGE, width), F32)
        padded[pl.ds(edge, EDGE), :] = jnp.zeros((EDGE, width), F32)
    for lanes in [slice(i, i + tile) for i in range(0, width, tile)]:
        conv_grad[pl.ds(EDGE, rows), lanes] = scale * (
            scaled[:, lanes] - sums - standard[:, lanes] * dots
        )
        padded[pl.ds(EDGE, rows), lanes] = glu[:, lanes].astype(F32)

    @pl.loop(0, width // 128)
    def _(step):
        lanes = pl.ds(pl.multiple_of(step * 128, 128), 128)
        place = pl.ds(pl.multiple_of(lax.rem(step, parts) * 128, 128), 128)
        value = conv_grad[pl.ds(EDGE, rows), lanes]
        for tap in range(tap_count):
            moved = padded[pl.ds(EDGE + tap - half_taps, rows), lanes]
            packet[step // parts, pl.ds(tap, 1), place] = jnp.sum(
                value * (masks[tap] * moved), axis=0, keepdims=True
            )


def taps(grad, panel, standard, inv_std, gain, glu, masks, loss):
    rows, width = standard.shape
    whole = pl.BlockSpec(memory_space=pltpu.HBM)
    vmem = pl.BlockSpec(memory_space=pltpu.VMEM)
    return pl.pallas_call(
        taps_kernel,
        out_shape=(
            jax.ShapeDtypeStruct((2, (masks.shape[0] + 9) // 8 * 8, width // 2), F32),
            jax.ShapeDtypeStruct((rows + 2 * EDGE, width), F32),
        ),
        in_specs=[vmem, whole, whole, vmem, vmem, whole, whole]
        + [pl.BlockSpec(memory_space=pltpu.SMEM)],
        out_specs=(vmem, vmem),
        scratch_shapes=[
            pltpu.VMEM((rows, width), F32),
            pltpu.VMEM((rows + 2 * EDGE, width), F32),
            pltpu.VMEM(panel.shape, BF16),
            pltpu.VMEM(standard.shape, F32),
            pltpu.VMEM(glu.shape, BF16),
            pltpu.VMEM(masks.shape, F32),
            pltpu.SemaphoreType.DMA((3 + width // 512,)),
        ],
        compiler_params=pltpu.CompilerParams(vmem_limit_bytes=60 << 20),
        cost_estimate=pl.CostEstimate(flops=1000, bytes_accessed=1000, transcendentals=0),
        name="taps",
    )(grad, panel, standard, inv_std, gain[None, :], glu, masks, loss)


def spread_kernel(conv_grad, kernel, masks, out):
    rows, width = out.shape
    tap_count = masks.shape[0]
    half_taps = tap_count // 2

    @pl.loop(0, width // 128)
    def _(step):
        lanes = pl.ds(pl.multiple_of(step * 128, 128), 128)
        total = jnp.zeros((rows, 128), F32)
        for tap in range(tap_count):
            moved = conv_grad[pl.ds(EDGE + half_taps - tap, rows), lanes]
            total = total + kernel[pl.ds(tap, 1), lanes] * (
                masks[tap_count - 1 - tap] * moved
            )
        out[:, lanes] = total.astype(BF16)


def spread(conv_grad, kernel, masks):
    vmem = pl.BlockSpec(memory_space=pltpu.VMEM)
    return pl.pallas_call(
        spread_kernel,
        out_shape=jax.ShapeDtypeStruct((conv_grad.shape[0] - 2 * EDGE, kernel.shape[1]), BF16),
        in_specs=[vmem] * 3,
        out_specs=vmem,
        compiler_params=pltpu.CompilerParams(vmem_limit_bytes=12 << 20),
        cost_estimate=pl.CostEstimate(flops=6_000_000_000, bytes_accessed=3_000_000, transcendentals=0),
        name="spread",
    )(conv_grad, kernel, masks)


def local(
    glu_frames,
    residual_frames,
    send_rows,
    recv_slot,
    segment_ids,
    code_targets,
    conv_kernel,
    norm_gain,
    point_weight,
    code_head,
):
    n_dp, n_fsdp = lax.axis_size("dp"), lax.axis_size("fsdp")
    d, f = lax.axis_index("dp"), lax.axis_index("fsdp")
    feature_width = glu_frames.shape[1]
    tap_count = conv_kernel.shape[0]
    half_taps = tap_count // 2
    slot_list = recv_slot[0, 0]
    row_count = slot_list.shape[0]
    picked_rows = send_rows[0, 0]

    capacity = picked_rows.shape[1]
    sent = jnp.concatenate([glu_frames[picked_rows], residual_frames[picked_rows]], axis=1)
    received = lax.all_to_all(sent, "dp", split_axis=0, concat_axis=0, tiled=True)
    segments = segment_ids[0, 0]
    seg_pad = jnp.pad(segments, (half_taps, half_taps), constant_values=-1)
    masks = jnp.stack(
        [seg_pad[offset : offset + row_count] == segments for offset in range(tap_count)]
    )
    masks = jnp.broadcast_to(masks.astype(F32)[:, :, None], (*masks.shape, 128))
    glu_owned, residual_owned, standard, inv_std, activation = forward(
        received, slot_list, masks, conv_kernel, norm_gain
    )

    pieces = gather_point(point_weight, d, activation)
    full_panel, residual_new = branch(
        point_weight, activation, residual_owned, pieces, d, f
    )

    code_local = code_head.shape[1]
    targets = code_targets[0].reshape(n_fsdp, row_count) - f * code_local
    columns = lax.broadcasted_iota(jnp.int32, (1, code_local), 1)
    gathered = gather_rows(residual_new, f)
    logits, hits, stats = {}, {}, {}
    act_own = after(activation, residual_new)
    acts = {mask: flip_dp(act_own, mask) if mask else act_own for mask in range(0, n_dp, 2)}
    acts.update({mask + 1: flip_dp(act, 1) for mask, act in list(acts.items())})
    gathered[-1] = (gathered[-1][0], after(gathered[-1][1], *acts.values()))
    for distance, block in gathered:
        logits[distance] = jnp.dot(block, code_head, preferred_element_type=F32)
        hits[distance] = pick(targets, (f + distance) % n_fsdp)[:, None] == columns
        top = jnp.max(logits[distance], axis=1)
        total = jnp.sum(jnp.exp(logits[distance] - top[:, None]), axis=1)
        chosen = jnp.sum(jnp.where(hits[distance], logits[distance], 0.0), axis=1)
        stats[distance] = jnp.stack([top, total, chosen])
    places = jnp.arange(n_fsdp)[:, None, None]
    table = tree_sum(
        [
            jnp.where(places == (f + distance) % n_fsdp, stats[distance], 0.0)
            for distance, _ in gathered
        ]
    )
    tables = [table] + [flip_fsdp(table, mask) for mask in range(1, n_fsdp)]
    tops = tables[0][:, 0]
    for other in tables[1:]:
        tops = jnp.maximum(tops, other[:, 0])
    sums = tree_sum([t[:, 1] * jnp.exp(t[:, 0] - tops) for t in tables])
    log_norm = tops + jnp.log(sums)
    loss_part = jnp.sum(log_norm - tree_sum([t[:, 2] for t in tables]))

    def code_part(distances, dtype):
        index = jnp.stack([(f + distance) % n_fsdp for distance in distances])
        return code_grad(
            [logits[distance] for distance in distances],
            index,
            log_norm,
            targets,
            code_head,
            dtype,
        )

    grad_residual, sides = scatter_rows(code_part, gathered, d, f)
    grad_residual, turned = lax.optimization_barrier(
        (grad_residual.astype(BF16), grad_residual.astype(BF16).T)
    )

    part_width = feature_width // n_dp
    cols = lax.all_to_all(
        turned.reshape(n_dp, part_width, row_count),
        "dp",
        split_axis=0,
        concat_axis=0,
        tiled=True,
    )
    packet, conv_grad = taps(
        grad_residual,
        full_panel,
        standard,
        inv_std,
        norm_gain,
        glu_owned,
        masks,
        loss_part.reshape(1, 1),
    )

    core = d & 1
    packet = after(packet, cols)
    packet = pick(packet, core) + flip_dp(pick(packet, 1 - core).astype(BF16), 1).astype(F32)
    packet = packet.astype(BF16)
    cols = after(cols, packet)
    point_own, point_sent = point_part(cols, [acts[mask] for mask in range(n_dp)], d, f)
    sides = [(keep, after(other, point_sent), left) for keep, other, left in sides]
    sides = middle_folds(sides, d)
    ready = [keep for keep, _, _ in sides]
    others = [after(flip_dp(packet, mask), *ready) for mask in range(2, n_dp, 2)]
    packet = tree_sum([packet.astype(F32)] + [other.astype(F32) for other in others])
    packet = packet.astype(BF16)
    grad_point = tree_sum(
        [point_own]
        + [flip_fsdp(point_sent[mask], mask).astype(F32) for mask in range(1, n_fsdp)]
    ).T
    grad_glu = spread(after(conv_grad, packet), conv_kernel, masks)
    grad_head = last_fold([after(part, packet) for keep, other, _ in sides for part in (keep, other)])
    others = [
        after(flip_fsdp(packet, mask), grad_glu, grad_head) for mask in range(1, n_fsdp)
    ]
    packet = tree_sum([packet.astype(F32)] + [other.astype(F32) for other in others])
    packet = ordered(core, packet, flip_dp(packet, 1), 1).reshape(-1, feature_width)
    loss = packet[tap_count + 1, 0] / (row_count * n_dp * n_fsdp * n_fsdp)
    return (
        loss,
        grad_head,
        grad_point,
        packet[:tap_count],
        packet[tap_count],
        grad_residual,
        grad_glu,
    )


def solution(mesh):
    placed = (
        P(("dp", "fsdp"), None),
        P(("dp", "fsdp"), None),
        P("dp", "fsdp", None, None),
        P("dp", "fsdp", None),
        P("dp", "fsdp", None),
        P("dp", None),
        P(),
        P(),
        P("fsdp", None),
        P(None, "fsdp"),
    )
    return jax.shard_map(
        local,
        mesh=mesh,
        in_specs=placed,
        out_specs=(
            P(),
            P("dp", "fsdp"),
            P("fsdp", "dp"),
            P(),
            P(),
            P(("dp", "fsdp"), None),
            P(("dp", "fsdp"), None),
        ),
        check_vma=False,
    )
```

profile of v0, /device:TPU:0, one launch (start us, length us, event | category | flops | bytes accessed | tf_op | source)
XLA Modules:
  0.0 213.2 jit_solution(2140386953875370190)
XLA Ops:
  2.9 3.0 %collective-permute-start = (bf16[2,48,1536]{2,1,0:T(8,128)(2,1)}, bf16[2,48,1536]{2,1,0:T(8,128)(2,1)S(1)}, u32[]{:S(2)}, u32[]{:S(2)}) collective-permute-start(bf16[2,48,1536]{2,1,0:T(8,128)(2,1)} %pad_maximum_fusion.2), channel_id=1, source_target_pairs={{0,1},{1,2},{2,3},{3,0},{4,5},{5,6},{6,7},{7,4},{8,9},{9,10},{10,1... | collective-permute-start | bytes 884744 | tf_op jit(solution)/shard_map/ppermute | solution.py:26
  13.8 3.9 %all-to-all-start = ((bf16[8,64,1536]{2,1,0:T(8,128)(2,1)}), bf16[8,64,1536]{2,1,0:T(8,128)(2,1)S(1)}, u32[]{:S(2)}, u32[]{:S(2)}) async-start(bf16[8,64,1536]{2,1,0:T(8,128)(2,1)} %pad_maximum_fusion), calls=%async_computation | async-start | bytes 3145728 | tf_op jit(solution)/shard_map/all_to_all | solution.py:659
  17.7 10.3 %collective-permute-done.1 = bf16[2,48,1536]{2,1,0:T(8,128)(2,1)} collective-permute-done((bf16[2,48,1536]{2,1,0:T(8,128)(2,1)}, bf16[2,48,1536]{2,1,0:T(8,128)(2,1)}, u32[]{:S(2)}, u32[]{:S(2)}) %collective-permute-start.1) | collective-permute-done | bytes 294944 | tf_op jit(solution)/shard_map/ppermute | solution.py:26
  35.0 4.2 %all-to-all-done.sent = bf16[8,64,1536]{2,1,0:T(8,128)(2,1)S(1)} async-done(((bf16[8,64,1536]{2,1,0:T(8,128)(2,1)}), bf16[8,64,1536]{2,1,0:T(8,128)(2,1)S(1)}, u32[]{:S(2)}, u32[]{:S(2)}) %all-to-all-start) | async-done | bytes 1572896 | tf_op jit(solution)/shard_map/all_to_all | solution.py:659
  41.1 8.2 %forward.1 = (bf16[128,1536]{1,0:T(8,128)(2,1)}, bf16[128,1536]{1,0:T(8,128)(2,1)}, f32[128,1536]{1,0:T(8,128)}, f32[128,1]{1,0:T(8,128)}, bf16[128,1536]{1,0:T(8,128)(2,1)}) custom-call(bf16[8,64,1536]{2,1,0:T(8,128)(2,1)} %copy-done.12, s32[128,1]{1,0:T(8,128)} %copy.22.slots, f32[31,128,128]{2,1,0:T(8,128)} %broadcast_in_dim.81.masks, f32[31,1536]{1,0:T(8,128)} %kernel.3, ...), custom_call_target="tpu_custom_call" | custom-call | flops 1000000000 | bytes 6000000 | tf_op jit(solution)/shard_map/forward/pallas_call | solution.py:189
  52.8 6.6 %branch.1 = (bf16[4,2,2,2,48,1536]{5,4,3,2,1,0:T(8,128)(2,1)}, bf16[128,1536]{1,0:T(8,128)(2,1)}) custom-call(s32[2]{0:T(128)} %pad_add_fusion.1.place, bf16[2,2,2,48,1536]{4,3,2,1,0:T(8,128)(2,1)} %bitcast.238, bf16[128,1536]{1,0:T(8,128)(2,1)} %get-tuple-element.68.act.refs_0_, bf16[128,1536]{1,0:T(8,128)(2,1)} %get-tuple-element.64.residual, ...), custom_call_target="tpu_custom_call" | custom-call | tf_op jit(solution)/shard_map/branch/pallas_call | solution.py:106
  66.9 4.0 %fusion.32 = (f32[128]{0:T(128)S(1)}, f32[128,2048]{1,0:T(8,128)S(1)}) fusion(bf16[128,1536]{1,0:T(8,128)(2,1)} %get-tuple-element.67.refs_0_, bf16[1536,2048]{1,0:T(8,128)(2,1)} %refs_1_.1), kind=kOutput, calls=%fused_computation.156 | convolution fusion | flops 805568384 | bytes 7733760 | tf_op jit(solution)/shard_map/dot_general | solution.py:685
  73.5 7.7 %collective-permute-done.9.refs_2_ = bf16[128,1536]{1,0:T(8,128)(2,1)S(1)} collective-permute-done((bf16[128,1536]{1,0:T(8,128)(2,1)}, bf16[128,1536]{1,0:T(8,128)(2,1)S(1)}, u32[]{:S(2)}, u32[]{:S(2)}) %collective-permute-start.9) | collective-permute-done | bytes 393248 | tf_op jit(solution)/shard_map/ppermute | solution.py:26
  87.3 5.3 %collective-permute-done.10.refs_3_ = bf16[128,1536]{1,0:T(8,128)(2,1)S(1)} collective-permute-done((bf16[128,1536]{1,0:T(8,128)(2,1)S(1)}, bf16[128,1536]{1,0:T(8,128)(2,1)S(1)}, u32[]{:S(2)}, u32[]{:S(2)}) %collective-permute-start.10) | collective-permute-done | bytes 393248 | tf_op jit(solution)/shard_map/ppermute | solution.py:377
  102.7 3.3 %code.3 = (bf16[128,2048]{1,0:T(8,128)(2,1)S(1)}, bf16[128,1536]{1,0:T(8,128)(2,1)S(1)}) custom-call(s32[1]{0:T(128)} %bitcast.77.index, f32[4,128]{1,0:T(4,128)S(1)} %get-tuple-element.128.norms, f32[4,128]{1,0:T(4,128)S(1)} %convert_element_type.79.targets, f32[128,2048]{1,0:T(8,128)S(1)} %get-tuple-element.173.refs_0_, bf16[1536,2048]{1,0:T(8,128)(2,1)S(1)} %bitcast.227), custom_call_target="tpu_custom_call" | custom-call | flops 800000000 | bytes 8000000 | tf_op jit(solution)/shard_map/code/pallas_call | solution.py:257
  106.2 4.8 %code.2 = (bf16[128,2048]{1,0:T(8,128)(2,1)S(1)}, bf16[128,2048]{1,0:T(8,128)(2,1)S(1)}, bf16[128,2048]{1,0:T(8,128)(2,1)S(1)}, f32[128,1536]{1,0:T(8,128)S(1)},...) custom-call(s32[3]{0:T(128)S(1)} %pad_add_fusion.index, f32[4,128]{1,0:T(4,128)S(1)} %get-tuple-element.128.norms, ...), custom_call_target="tpu_custom_call" | custom-call | flops 2400000000 | bytes 8000000 | tf_op jit(solution)/shard_map/code/pallas_call | solution.py:257
  111.0 3.9 %collective-permute-done.21 = bf16[128,1536]{1,0:T(8,128)(2,1)S(1)} collective-permute-done((bf16[128,1536]{1,0:T(8,128)(2,1)S(1)}, bf16[128,1536]{1,0:T(8,128)(2,1)S(1)}, u32[]{:S(2)}, u32[]{:S(2)}) %collective-permute-start.21) | collective-permute-done | bytes 393248 | tf_op jit(solution)/shard_map/ppermute | solution.py:396
  115.8 8.5 %head.1 = (bf16[4,192,2048]{2,1,0:T(8,128)(2,1)S(1)}, bf16[4,192,2048]{2,1,0:T(8,128)(2,1)}) custom-call(s32[1]{0:T(128)} %bitcast.80.place, bf16[128,1536]{1,0:T(8,128)(2,1)S(1)} %copy-done.5, bf16[128,1536]{1,0:T(8,128)(2,1)S(1)} %collective-permute-done.8.refs_1_, bf16[128,1536]{1,0:T(8,128)(2,1)S(1)} %collective-permute-done.9.refs_2_, ...), custom_call_target="tpu_custom_call" | custom-call | flops 1000 | bytes 1000 | tf_op jit(solution)/shard_map/head/pallas_call | solution.py:313
  126.0 3.8 %collective-permute-start.24 = (bf16[128,1536]{1,0:T(8,128)(2,1)S(1)}, bf16[128,1536]{1,0:T(8,128)(2,1)}, u32[]{:S(2)}, u32[]{:S(2)}) collective-permute-start(bf16[128,1536]{1,0:T(8,128)(2,1)S(1)} %get-tuple-element.137), channel_id=1, source_target_pairs={{0,3},{1,0},{2,1},{3,2},{4,7},{5,4},{6,5},{7,6},{8,11},{9,8},{10,9... | collective-permute-start | bytes 1179656 | tf_op jit(solution)/shard_map/ppermute | solution.py:26
  133.8 3.2 %fold.2 = (bf16[2,1,192,1024]{3,2,1,0:T(8,128)(2,1)S(1)}, bf16[2,1,192,1024]{3,2,1,0:T(8,128)(2,1)S(1)}, bf16[1,2,192,1024]{3,2,1,0:T(8,128)(2,1)S(1)}, bf16[1,2,192,1024]{3,2,1,0:T(8,128)(2,1)S(1)}) custom-call(s32[2]{0:T(128)S(1)} %pad_add_fusion.2.place, bf16[2,2,1,192,2048]{4,3,2,1,0:T(8,128)(2,1)S(1)} %bitcast.228, ...), custom_call_target="tpu_custom_call" | custom-call | flops 1000 | bytes 1000 | tf_op jit(solution)/shard_map/fold/pallas_call | solution.py:444
  137.0 3.0 %collective-permute-done.22 = bf16[128,1536]{1,0:T(8,128)(2,1)} collective-permute-done((bf16[128,1536]{1,0:T(8,128)(2,1)}, bf16[128,1536]{1,0:T(8,128)(2,1)}, u32[]{:S(2)}, u32[]{:S(2)}) %collective-permute-start.22) | collective-permute-done | bytes 393248 | tf_op jit(solution)/shard_map/ppermute | solution.py:26
  140.0 6.0 %collective-permute-done.24 = bf16[128,1536]{1,0:T(8,128)(2,1)} collective-permute-done((bf16[128,1536]{1,0:T(8,128)(2,1)S(1)}, bf16[128,1536]{1,0:T(8,128)(2,1)}, u32[]{:S(2)}, u32[]{:S(2)}) %collective-permute-start.24) | collective-permute-done | bytes 393248 | tf_op jit(solution)/shard_map/ppermute | solution.py:26
  148.3 3.5 %all-to-all-start.1 = ((bf16[8,192,128]{2,1,0:T(8,128)(2,1)}), bf16[8,192,128]{2,1,0:T(8,128)(2,1)S(1)}, u32[]{:S(2)}, u32[]{:S(2)}) async-start(bf16[8,192,128]{2,1,0:T(8,128)(2,1)} %bitcast.89), calls=%async_computation.1 | async-start | bytes 786432 | tf_op jit(solution)/shard_map/all_to_all | solution.py:723
  155.2 11.1 %taps.1 = (f32[2,40,768]{2,1,0:T(8,128)}, f32[160,1536]{1,0:T(8,128)}) custom-call(bf16[128,1536]{1,0:T(8,128)(2,1)} %copy-done.13, bf16[1536,1536]{1,0:T(8,128)(2,1)} %bitcast.237, f32[128,1536]{1,0:T(8,128)} %get-tuple-element.90.standard, f32[128,1]{1,0:T(8,128)} %get-tuple-element.91.inv_std, f32[1,1536]{1,0:T(1,128)} %broadcast_in_dim.82.gain, ...), custom_call_target="tpu_custom_call" | custom-call | flops 1000 | bytes 1000 | tf_op jit(solution)/shard_map/taps/pallas_call | solution.py:582
  170.4 2.8 %collective-permute-start.30 = (bf16[40,768]{1,0:T(8,128)(2,1)S(1)}, bf16[40,768]{1,0:T(8,128)(2,1)S(1)}, u32[]{:S(2)}, u32[]{:S(2)}) collective-permute-start(bf16[40,768]{1,0:T(8,128)(2,1)S(1)} %fusion.8), channel_id=1, source_target_pairs={{0,24},{4,28},{8,16},{12,20},{16,8},{20,12},{24,0},{28,4},{1,25},{... | collective-permute-start | bytes 184328 | tf_op jit(solution)/shard_map/ppermute | solution.py:16
  173.2 5.2 %point.1 = (f32[192,384]{1,0:T(8,128)}, bf16[4,192,384]{2,1,0:T(8,128)(2,1)}) custom-call(s32[2]{0:T(128)} %pad_add_fusion.1.place, bf16[8,192,128]{2,1,0:T(8,128)(2,1)} %copy-done.15, bf16[128,1536]{1,0:T(8,128)(2,1)} %get-tuple-element.68.act.refs_0_, bf16[128,1536]{1,0:T(8,128)(2,1)} %copy-done.22, bf16[128,1536]{1,0:T(8,128)(2,1)} %copy-done.19, ...), custom_call_target="tpu_custom_call" | custom-call | flops 1000 | bytes 1000 | tf_op jit(solution)/shard_map/point/pallas_call | solution.py:350
  187.0 4.6 %spread.1 = bf16[128,1536]{1,0:T(8,128)(2,1)} custom-call(f32[160,1536]{1,0:T(8,128)S(1)} %copy-done.7, f32[31,1536]{1,0:T(8,128)S(1)} %copy-done.6, f32[31,128,128]{2,1,0:T(8,128)S(1)} %copy-done.2), custom_call_target="tpu_custom_call" | custom-call | flops 6000000000 | bytes 3000000 | tf_op jit(solution)/shard_map/spread/pallas_call | solution.py:625
  191.7 4.2 %collective-permute-done.33 = bf16[1,1,192,1024]{3,2,1,0:T(8,128)(2,1)S(1)} collective-permute-done((bf16[1,1,192,1024]{3,2,1,0:T(8,128)(2,1)S(1)}, bf16[1,1,192,1024]{3,2,1,0:T(8,128)(2,1)S(1)}, u32[]{:S(2)}, u32[]{:S(2)}) %collective-permute-start.33) | collective-permute-done | bytes 393248 | tf_op jit(solution)/shard_map/ppermute | solution.py:16
  201.7 6.8 %collective-permute-done.38 = bf16[192,384]{1,0:T(8,128)(2,1)S(1)} collective-permute-done((bf16[192,384]{1,0:T(8,128)(2,1)S(1)}, bf16[192,384]{1,0:T(8,128)(2,1)S(1)}, u32[]{:S(2)}, u32[]{:S(2)}) %collective-permute-start.38) | collective-permute-done | bytes 147488 | tf_op jit(solution)/shard_map/ppermute | solution.py:21
  (202 shorter events, 82.3 us)
Async XLA Ops:
  2.9 14.9 %collective-permute-start = (bf16[2,48,1536]{2,1,0:T(8,128)(2,1)}, bf16[2,48,1536]{2,1,0:T(8,128)(2,1)S(1)}, u32[]{:S(2)}, u32[]{:S(2)}) collective-permute-start(bf16[2,48,1536]{2,1,0:T(8,128)(2,1)} %pad_maximum_fusion.2), channel_id=1, source_target_pairs={{0,1},{1,2},{2,3},{3,0},{4,5},{5,6},{6,7},{7,4},{8,9},{9,10},{10,1... | collective-permute-start | bytes 884744 | tf_op jit(solution)/shard_map/ppermute | solution.py:26
  5.9 22.1 %collective-permute-start.1 = (bf16[2,48,1536]{2,1,0:T(8,128)(2,1)}, bf16[2,48,1536]{2,1,0:T(8,128)(2,1)}, u32[]{:S(2)}, u32[]{:S(2)}) collective-permute-start(bf16[2,48,1536]{2,1,0:T(8,128)(2,1)} %pad_maximum_fusion.2), channel_id=1, source_target_pairs={{0,2},{1,3},{2,0},{3,1},{4,6},{5,7},{6,4},{7,5},{8,10},{9,11},{10,... | collective-permute-start | bytes 884744 | tf_op jit(solution)/shard_map/ppermute | solution.py:26
  8.5 19.5 %collective-permute-start.2 = (bf16[2,48,1536]{2,1,0:T(8,128)(2,1)}, bf16[2,48,1536]{2,1,0:T(8,128)(2,1)}, u32[]{:S(2)}, u32[]{:S(2)}) collective-permute-start(bf16[2,48,1536]{2,1,0:T(8,128)(2,1)} %pad_maximum_fusion.2), channel_id=1, source_target_pairs={{0,3},{1,0},{2,1},{3,2},{4,7},{5,4},{6,5},{7,6},{8,11},{9,8},{10,9... | collective-permute-start | bytes 884744 | tf_op jit(solution)/shard_map/ppermute | solution.py:26
  13.8 25.4 %all-to-all-start = ((bf16[8,64,1536]{2,1,0:T(8,128)(2,1)}), bf16[8,64,1536]{2,1,0:T(8,128)(2,1)S(1)}, u32[]{:S(2)}, u32[]{:S(2)}) async-start(bf16[8,64,1536]{2,1,0:T(8,128)(2,1)} %pad_maximum_fusion), calls=%async_computation | async-start | bytes 3145728 | tf_op jit(solution)/shard_map/all_to_all | solution.py:659
  29.2 21.3 %collective-permute-start.5 = (bf16[2,3,48,1536]{3,2,1,0:T(8,128)(2,1)S(1)}, bf16[2,3,48,1536]{3,2,1,0:T(8,128)(2,1)}, u32[]{:S(2)}, u32[]{:S(2)}) collective-permute-start(bf16[2,3,48,1536]{3,2,1,0:T(8,128)(2,1)S(1)} %pad_maximum_fusion.1.got), channel_id=1, source_target_pairs={{0,4},{4,0},{8,12},{12,8},{16,20},{20,16},{24,28},{28,24},{1,5},{5... | collective-permute-start | bytes 2654216 | tf_op jit(solution)/shard_map/ppermute | solution.py:16
  30.4 18.9 %collective-permute-start.4 = (bf16[3,48,1536]{2,1,0:T(8,128)(2,1)}, bf16[3,48,1536]{2,1,0:T(8,128)(2,1)S(1)}, u32[]{:S(2)}, u32[]{:S(2)}) collective-permute-start(bf16[3,48,1536]{2,1,0:T(8,128)(2,1)} %get-tuple-element.131), channel_id=1, source_target_pairs={{0,16},{4,20},{8,24},{12,28},{16,0},{20,4},{24,8},{28,12},{1,17},{... | collective-permute-start | bytes 1327112 | tf_op jit(solution)/shard_map/ppermute | solution.py:16
  31.9 17.5 %collective-permute-start.3 = (bf16[3,48,1536]{2,1,0:T(8,128)(2,1)}, bf16[3,48,1536]{2,1,0:T(8,128)(2,1)}, u32[]{:S(2)}, u32[]{:S(2)}) collective-permute-start(bf16[3,48,1536]{2,1,0:T(8,128)(2,1)} %get-tuple-element.132), channel_id=1, source_target_pairs={{0,8},{4,12},{8,0},{12,4},{16,24},{20,28},{24,16},{28,20},{1,9},{5... | collective-permute-start | bytes 1327112 | tf_op jit(solution)/shard_map/ppermute | solution.py:16
  59.5 14.1 %collective-permute-start.8 = (bf16[128,1536]{1,0:T(8,128)(2,1)}, bf16[128,1536]{1,0:T(8,128)(2,1)S(1)}, u32[]{:S(2)}, u32[]{:S(2)}) collective-permute-start(bf16[128,1536]{1,0:T(8,128)(2,1)} %get-tuple-element.67.refs_0_), channel_id=1, source_target_pairs={{0,1},{1,2},{2,3},{3,0},{4,5},{5,6},{6,7},{7,4},{8,9},{9,10},{10,1... | collective-permute-start | bytes 1179656 | tf_op jit(solution)/shard_map/ppermute | solution.py:26
  62.1 19.1 %collective-permute-start.9 = (bf16[128,1536]{1,0:T(8,128)(2,1)}, bf16[128,1536]{1,0:T(8,128)(2,1)S(1)}, u32[]{:S(2)}, u32[]{:S(2)}) collective-permute-start(bf16[128,1536]{1,0:T(8,128)(2,1)} %get-tuple-element.67.refs_0_), channel_id=1, source_target_pairs={{0,3},{1,0},{2,1},{3,2},{4,7},{5,4},{6,5},{7,6},{8,11},{9,8},{10,9... | collective-permute-start | bytes 1179656 | tf_op jit(solution)/shard_map/ppermute | solution.py:26
  63.4 19.9 %collective-permute-start.11 = (bf16[128,1536]{1,0:T(8,128)(2,1)S(1)}, bf16[128,1536]{1,0:T(8,128)(2,1)S(1)}, u32[]{:S(2)}, u32[]{:S(2)}) collective-permute-start(bf16[128,1536]{1,0:T(8,128)(2,1)S(1)} %copy-done.14), channel_id=1, source_target_pairs={{0,8},{4,12},{8,0},{12,4},{16,24},{20,28},{24,16},{28,20},{1,9},{5... | collective-permute-start | bytes 1179656 | tf_op jit(solution)/shard_map/ppermute | solution.py:16
  63.8 20.0 %collective-permute-start.12 = (bf16[128,1536]{1,0:T(8,128)(2,1)S(1)}, bf16[128,1536]{1,0:T(8,128)(2,1)S(1)}, u32[]{:S(2)}, u32[]{:S(2)}) collective-permute-start(bf16[128,1536]{1,0:T(8,128)(2,1)S(1)} %copy-done.14), channel_id=1, source_target_pairs={{0,16},{4,20},{8,24},{12,28},{16,0},{20,4},{24,8},{28,12},{1,17},{... | collective-permute-start | bytes 1179656 | tf_op jit(solution)/shard_map/ppermute | solution.py:16
  64.5 21.0 %collective-permute-start.13 = (bf16[128,1536]{1,0:T(8,128)(2,1)S(1)}, bf16[128,1536]{1,0:T(8,128)(2,1)S(1)}, u32[]{:S(2)}, u32[]{:S(2)}) collective-permute-start(bf16[128,1536]{1,0:T(8,128)(2,1)S(1)} %copy-done.14), channel_id=1, source_target_pairs={{0,24},{4,28},{8,16},{12,20},{16,8},{20,12},{24,0},{28,4},{1,25},{... | collective-permute-start | bytes 1179656 | tf_op jit(solution)/shard_map/ppermute | solution.py:16
  73.5 12.5 %collective-permute-start.14 = (bf16[128,1536]{1,0:T(8,128)(2,1)S(1)}, bf16[128,1536]{1,0:T(8,128)(2,1)S(1)}, u32[]{:S(2)}, u32[]{:S(2)}) collective-permute-start(bf16[128,1536]{1,0:T(8,128)(2,1)S(1)} %copy-done.14), channel_id=1, source_target_pairs={{0,4},{4,0},{8,12},{12,8},{16,20},{20,16},{24,28},{28,24},{1,5},{5... | collective-permute-start | bytes 1179656 | tf_op jit(solution)/shard_map/ppermute | solution.py:16
  125.9 14.1 %collective-permute-start.22 = (bf16[128,1536]{1,0:T(8,128)(2,1)}, bf16[128,1536]{1,0:T(8,128)(2,1)}, u32[]{:S(2)}, u32[]{:S(2)}) collective-permute-start(bf16[128,1536]{1,0:T(8,128)(2,1)} %get-tuple-element.136), channel_id=1, source_target_pairs={{0,1},{1,2},{2,3},{3,0},{4,5},{5,6},{6,7},{7,4},{8,9},{9,10},{10,1... | collective-permute-start | bytes 1179656 | tf_op jit(solution)/shard_map/ppermute | solution.py:26
  126.0 20.1 %collective-permute-start.24 = (bf16[128,1536]{1,0:T(8,128)(2,1)S(1)}, bf16[128,1536]{1,0:T(8,128)(2,1)}, u32[]{:S(2)}, u32[]{:S(2)}) collective-permute-start(bf16[128,1536]{1,0:T(8,128)(2,1)S(1)} %get-tuple-element.137), channel_id=1, source_target_pairs={{0,3},{1,0},{2,1},{3,2},{4,7},{5,4},{6,5},{7,6},{8,11},{9,8},{10,9... | collective-permute-start | bytes 1179656 | tf_op jit(solution)/shard_map/ppermute | solution.py:26
  148.3 18.0 %all-to-all-start.1 = ((bf16[8,192,128]{2,1,0:T(8,128)(2,1)}), bf16[8,192,128]{2,1,0:T(8,128)(2,1)S(1)}, u32[]{:S(2)}, u32[]{:S(2)}) async-start(bf16[8,192,128]{2,1,0:T(8,128)(2,1)} %bitcast.89), calls=%async_computation.1 | async-start | bytes 786432 | tf_op jit(solution)/shard_map/all_to_all | solution.py:723
  151.8 27.8 %collective-permute-start.28 = (bf16[1,2,192,1024]{3,2,1,0:T(8,128)(2,1)}, bf16[1,2,192,1024]{3,2,1,0:T(8,128)(2,1)}, u32[]{:S(2)}, u32[]{:S(2)}) collective-permute-start(bf16[1,2,192,1024]{3,2,1,0:T(8,128)(2,1)} %copy-done.9), channel_id=1, source_target_pairs={{0,16},{4,20},{8,24},{12,28},{16,0},{20,4},{24,8},{28,12},{1,17},{... | collective-permute-start | bytes 2359304 | tf_op jit(solution)/shard_map/ppermute | solution.py:16
  153.7 25.9 %collective-permute-start.27 = (bf16[2,1,192,1024]{3,2,0,1:T(8,128)(2,1)}, bf16[2,1,192,1024]{3,2,0,1:T(8,128)(2,1)}, u32[]{:S(2)}, u32[]{:S(2)}) collective-permute-start(bf16[2,1,192,1024]{3,2,0,1:T(8,128)(2,1)} %bitcast.236), channel_id=1, source_target_pairs={{0,8},{4,12},{8,0},{12,4},{16,24},{20,28},{24,16},{28,20},{1,9},{5... | collective-permute-start | bytes 2359304 | tf_op jit(solution)/shard_map/ppermute | solution.py:16
  169.6 12.2 %collective-permute-start.26 = (bf16[40,768]{1,0:T(8,128)(2,1)S(1)}, bf16[40,768]{1,0:T(8,128)(2,1)S(1)}, u32[]{:S(2)}, u32[]{:S(2)}) collective-permute-start(bf16[40,768]{1,0:T(8,128)(2,1)S(1)} %fusion.8), channel_id=1, source_target_pairs={{0,8},{4,12},{8,0},{12,4},{16,24},{20,28},{24,16},{28,20},{1,9},{5... | collective-permute-start | bytes 184328 | tf_op jit(solution)/shard_map/ppermute | solution.py:16
  170.2 11.6 %collective-permute-start.29 = (bf16[40,768]{1,0:T(8,128)(2,1)S(1)}, bf16[40,768]{1,0:T(8,128)(2,1)S(1)}, u32[]{:S(2)}, u32[]{:S(2)}) collective-permute-start(bf16[40,768]{1,0:T(8,128)(2,1)S(1)} %fusion.8), channel_id=1, source_target_pairs={{0,16},{4,20},{8,24},{12,28},{16,0},{20,4},{24,8},{28,12},{1,17},{... | collective-permute-start | bytes 184328 | tf_op jit(solution)/shard_map/ppermute | solution.py:16
  181.9 18.6 %collective-permute-start.31 = (bf16[40,768]{1,0:T(8,128)(2,1)S(1)}, bf16[40,768]{1,0:T(8,128)(2,1)S(1)}, u32[]{:S(2)}, u32[]{:S(2)}) collective-permute-start(bf16[40,768]{1,0:T(8,128)(2,1)S(1)} %add_convert_fusion), channel_id=1, source_target_pairs={{0,1},{1,0},{2,3},{3,2},{4,5},{5,4},{6,7},{7,6},{8,9},{9,8},{10,11... | collective-permute-start | bytes 184328 | tf_op jit(solution)/shard_map/ppermute | solution.py:21
  183.6 17.9 %collective-permute-start.34 = (bf16[40,768]{1,0:T(8,128)(2,1)S(1)}, bf16[40,768]{1,0:T(8,128)(2,1)S(1)}, u32[]{:S(2)}, u32[]{:S(2)}) collective-permute-start(bf16[40,768]{1,0:T(8,128)(2,1)S(1)} %add_convert_fusion), channel_id=1, source_target_pairs={{0,2},{1,3},{2,0},{3,1},{4,6},{5,7},{6,4},{7,5},{8,10},{9,11},{10,... | collective-permute-start | bytes 184328 | tf_op jit(solution)/shard_map/ppermute | solution.py:21
  185.3 16.2 %collective-permute-start.35 = (bf16[40,768]{1,0:T(8,128)(2,1)S(1)}, bf16[40,768]{1,0:T(8,128)(2,1)S(1)}, u32[]{:S(2)}, u32[]{:S(2)}) collective-permute-start(bf16[40,768]{1,0:T(8,128)(2,1)S(1)} %add_convert_fusion), channel_id=1, source_target_pairs={{0,3},{1,2},{2,1},{3,0},{4,7},{5,6},{6,5},{7,4},{8,11},{9,10},{10,... | collective-permute-start | bytes 184328 | tf_op jit(solution)/shard_map/ppermute | solution.py:21
  196.6 11.9 %collective-permute-start.38 = (bf16[192,384]{1,0:T(8,128)(2,1)S(1)}, bf16[192,384]{1,0:T(8,128)(2,1)S(1)}, u32[]{:S(2)}, u32[]{:S(2)}) collective-permute-start(bf16[192,384]{1,0:T(8,128)(2,1)S(1)} %get-tuple-element.135), channel_id=1, source_target_pairs={{0,2},{1,3},{2,0},{3,1},{4,6},{5,7},{6,4},{7,5},{8,10},{9,11},{10,... | collective-permute-start | bytes 442376 | tf_op jit(solution)/shard_map/ppermute | solution.py:21
  (52 other events, 447.2 us)
where the time goes:
time: 214 us; the launch traced here: 213 us
  waiting for transfers between devices  63 us (29%)
  Pallas kernels  59.1 us (28%)
  starting transfers between devices  51.7 us (24%)
  local copies, waits for them, and re-layouts  18.3 us (9%)
  other arithmetic  10.8 us (5%)
  matrix products  7.37 us (3%)
  between operations  3.13 us (1%)
    ppermute x7, waiting for transfers between devices, shift_fsdp(): lax.ppermute(value, 'fsdp', [(i, (i + step) % count) for i in range(count)])  29.2 us
    ppermute x22, starting transfers between devices, flip_dp(): return lax.ppermute(value, 'dp', [(i, i ^ mask) for i in range(count)])  15.6 us
    ppermute x7, starting transfers between devices, shift_fsdp(): lax.ppermute(value, 'fsdp', [(i, (i + step) % count) for i in range(count)])  14.7 us
    ppermute x9, starting transfers between devices, flip_fsdp(): return lax.ppermute(value, 'fsdp', [(i, i ^ mask) for i in range(count)])  13.2 us
    pallas_call x1, Pallas kernels, taps(): pl.pallas_call(taps_kernel, out_shape=(jax.ShapeDtypeStruct((2, (masks.sh...  11.1 us
    ppermute x9, waiting for transfers between devices, flip_fsdp(): return lax.ppermute(value, 'fsdp', [(i, i ^ mask) for i in range(count)])  10.2 us
    ppermute x22, waiting for transfers between devices, flip_dp(): return lax.ppermute(value, 'dp', [(i, i ^ mask) for i in range(count)])  10.2 us
    pallas_call x1, Pallas kernels, head_grad(): pl.pallas_call(functools.partial(head_kernel, count), out_shape=(half, ha...  8.5 us
  transfers between devices with their start and end apart: 42, of which 17 were waited for; matrix products, arithmetic and copies ran while one was open for 10% of the time, Pallas kernels for 19%

commit v1 on v0

--- a/solution.py
+++ b/solution.py
@@ -278,69 +278,28 @@
     return made[:count], made[count:]
 
 
-def head_kernel(count, place, *refs):
-    rows, grads, mine, sent = refs[:count], refs[count : 2 * count], refs[-2], refs[-1]
-    core = place[0]
-    pairs, height, codes = mine.shape
-    tile = min(512, codes)
-    for pair in range(pairs):
-        side = slice(2 * pair * height, (2 * pair + 2) * height)
-        turned = jnp.concatenate([block[:, side] for block in rows]).T
-        for step in range(codes // tile):
-            lanes = slice(step * tile, (step + 1) * tile)
-            product = jnp.dot(
-                turned,
-                jnp.concatenate([grad[:, lanes] for grad in grads]),
-                preferred_element_type=F32,
-            ).astype(BF16)
-
-            @pl.when(core == 0)
-            def _():
-                mine[pair, :, lanes] = product[:height]
-                sent[pair, :, lanes] = product[height:]
-
-            @pl.when(core != 0)
-            def _():
-                mine[pair, :, lanes] = product[height:]
-                sent[pair, :, lanes] = product[:height]
-
-
-def head_grad(rows, grads, core):
-    n_dp = lax.axis_size("dp")
-    count = len(rows)
-    half = jax.ShapeDtypeStruct((n_dp // 2, rows[0].shape[1] // n_dp, grads[0].shape[1]), BF16)
-    vmem = pl.BlockSpec(memory_space=pltpu.VMEM)
-    return pl.pallas_call(
-        functools.partial(head_kernel, count),
-        out_shape=(half, half),
-        in_specs=[pl.BlockSpec(memory_space=pltpu.SMEM)] + [vmem] * (2 * count),
-        out_specs=(vmem, vmem),
-        compiler_params=pltpu.CompilerParams(vmem_limit_bytes=20 << 20),
-        cost_estimate=pl.CostEstimate(flops=1000, bytes_accessed=1000, transcendentals=0),
-        name="head",
-    )(core[None], *rows, *grads)
-
-
 def point_kernel(count, place, cols, *refs):
     given = refs[:count]
-    own, out, acts, parts, sems = refs[count:]
+    own, outs = refs[count], refs[count + 1 : -3]
+    acts, parts, sems = refs[-3:]
     d, f = place[0], place[1]
     copies = [pltpu.make_async_copy(given[i], acts.at[i], sems.at[i]) for i in range(count)]
     for copy in copies:
         copy.start()
     for copy in copies:
         copy.wait()
-    blocks, _, width = out.shape
+    blocks, _, width = parts.shape
     for block in range(blocks):
         lanes = slice(block * width, (block + 1) * width)
-        total = jnp.zeros(out.shape[1:], F32)
+        total = jnp.zeros(own.shape, F32)
         for mask in range(count):
             total = total + jnp.dot(
                 cols[d ^ mask], acts[mask, :, lanes], preferred_element_type=F32
             )
-        out[f ^ block] = total.astype(BF16)
         parts[block] = total
     own[...] = parts[f]
+    for i, out in enumerate(outs):
+        out[...] = parts[f ^ (i + 1)].astype(BF16)
 
 
 def point_part(cols, acts, d, f):
@@ -349,13 +308,11 @@
     vmem = pl.BlockSpec(memory_space=pltpu.VMEM)
     return pl.pallas_call(
         functools.partial(point_kernel, len(acts)),
-        out_shape=(
-            jax.ShapeDtypeStruct((cols.shape[1], width), F32),
-            jax.ShapeDtypeStruct((n_fsdp, cols.shape[1], width), BF16),
-        ),
+        out_shape=[jax.ShapeDtypeStruct((cols.shape[1], width), F32)]
+        + [jax.ShapeDtypeStruct((cols.shape[1], width), BF16)] * (n_fsdp - 1),
         in_specs=[pl.BlockSpec(memory_space=pltpu.SMEM), vmem]
         + [pl.BlockSpec(memory_space=pltpu.HBM)] * len(acts),
-        out_specs=(vmem, vmem),
+        out_specs=[vmem] * n_fsdp,
         scratch_shapes=[
             pltpu.VMEM((len(acts), *acts[0].shape), BF16),
             pltpu.VMEM((n_fsdp, cols.shape[1], width), F32),
@@ -383,14 +340,19 @@
 
     places = [distance for distance, _ in gathered]
 
-    def head_halves(grads):
-        return head_grad([block for _, block in gathered], [grads[p] for p in places], d & 1)
+    def head_grad(grads):
+        return lax.dot_general(
+            jnp.concatenate([block for _, block in gathered]),
+            jnp.concatenate([grads[place] for place in places]),
+            (((0,), (0,)), ((), ())),
+            preferred_element_type=F32,
+        ).astype(BF16)
 
     if count != 4:
         grads, outs = code_part(places, F32)
         grads, outs = dict(zip(places, grads)), dict(zip(places, outs))
         got = [shift_fsdp(outs[step].astype(BF16), step).astype(F32) for step in range(1, count)]
-        return sum(got, outs[0]), join_cores(*head_halves(grads), d)
+        return sum(got, outs[0]), join_cores(head_grad(grads), d)
     grads = {}
     (grads[2],), (block,) = code_part([2], BF16)
     across = lax.ppermute(block, "fsdp", [(2, 0), (1, 3), (3, 2), (0, 1)])
@@ -401,8 +363,8 @@
     got1 = shift_fsdp(ahead, 1)
     got2 = shift_fsdp(behind, -1)
     direct = jnp.where((f == 0) | (f == 3), across, 0.0)
-    mine, sent = head_halves({place: after(grads[place], ahead, behind) for place in places})
-    sides = join_cores(mine, sent, d)
+    head = head_grad({place: after(grads[place], ahead, behind) for place in places})
+    sides = join_cores(head, d)
     got1 = after(got1, *[keep for keep, _, _ in sides])
     return own + direct + got1.astype(F32) + got2.astype(F32), sides
 
@@ -413,7 +375,11 @@
     for i, (source, target) in enumerate(zip(ins, held)):
         if cut:
             width = target.shape[-1]
-            source = source.at[:, :, :, :, pl.ds(i // 2 * width, width)]
+            lanes = pl.ds(i // 2 * width, width)
+            if i % 2:
+                source = source.at[:, :, :, :, lanes]
+            else:
+                source = source.at[:, :, :, place[2], :, lanes]
         copies.append(pltpu.make_async_copy(source, target, sems.at[i]))
         copies[-1].start()
     for side in range(2):
@@ -433,10 +399,12 @@
     ins, outs, held, left_over = [], [], [], []
     for own, other, left, bit in sides:
         place = left.index(bit)
-        rows, width = own.shape[-2:]
+        rows, width = other.shape[-2:]
         part = width // 2 if cut else width
         before, behind = 2**place, 2 ** (len(left) - 1 - place)
-        ins += [value.reshape(before, 2, behind, rows, width) for value in (own, other)]
+        cores = (2,) if cut else ()
+        ins.append(own.reshape(before, 2, behind, *cores, rows, width))
+        ins.append(other.reshape(before, 2, behind, rows, width))
         held += [pltpu.VMEM((before, 2, behind, rows, part), BF16)] * 2
         outs += [jax.ShapeDtypeStruct((before, behind, rows, part), BF16)] * 2
         left_over.append([b for b in left if b != bit])
@@ -450,7 +418,7 @@
         compiler_params=pltpu.CompilerParams(vmem_limit_bytes=16 << 20),
         cost_estimate=pl.CostEstimate(flops=1000, bytes_accessed=1000, transcendentals=0),
         name="fold",
-    )(jnp.stack([(d >> side[3]) & 1 for side in sides]), *ins)
+    )(jnp.stack([(d >> side[3]) & 1 for side in sides] + [d & 1]), *ins)
     return [(made[2 * i], made[2 * i + 1], left_over[i]) for i in range(2)]
 
 
@@ -481,10 +449,12 @@
     return [list(range(1, bits))[step], list(range(bits - 1, 0, -1))[step]]
 
 
-def join_cores(mine, sent, d):
-    left = list(range(lax.axis_size("dp").bit_length() - 2, 0, -1))
-    got = flip_dp(sent, 1)
-    sides = [(mine, got, left, bit) for bit in halve_bits(0)]
+def join_cores(head, d):
+    count = lax.axis_size("dp")
+    left = list(range(count.bit_length() - 2, 0, -1))
+    cut = head.reshape(count // 2, 2, head.shape[0] // count, head.shape[1])
+    got = flip_dp(pick(cut, 1 - (d & 1), 1), 1)
+    sides = [(cut, got, left, bit) for bit in halve_bits(0)]
     return send_on(fold(sides, d, True), 0)
 
 
@@ -504,7 +474,7 @@
 
 
 def taps_kernel(
-    grad, panel, standard, inv_std, gain, glu, masks, loss, packet, conv_grad, scaled, padded, *held
+    grad, panel, standard, inv_std, gain, glu, masks, loss, place, mine, sent, conv_grad, scaled, padded, packet, *held
 ):
     rows, width = standard.shape
     tap_count = masks.shape[0]
@@ -543,8 +513,8 @@
         normed_grad = act_grad * sig * (1.0 + normed * (1.0 - sig))
         gain_grad = jnp.sum(normed_grad * unit, axis=0, keepdims=True)
         for first in range(0, tile, 128):
-            half, place = divmod(lanes.start + first, packet.shape[2])
-            packet[half, pl.ds(tap_count, 1), place : place + 128] = gain_grad[
+            half, first_lane = divmod(lanes.start + first, packet.shape[2])
+            packet[half, pl.ds(tap_count, 1), first_lane : first_lane + 128] = gain_grad[
                 :, first : first + 128
             ]
         part = normed_grad * scale
@@ -566,31 +536,37 @@
     @pl.loop(0, width // 128)
     def _(step):
         lanes = pl.ds(pl.multiple_of(step * 128, 128), 128)
-        place = pl.ds(pl.multiple_of(lax.rem(step, parts) * 128, 128), 128)
+        there = pl.ds(pl.multiple_of(lax.rem(step, parts) * 128, 128), 128)
         value = conv_grad[pl.ds(EDGE, rows), lanes]
         for tap in range(tap_count):
             moved = padded[pl.ds(EDGE + tap - half_taps, rows), lanes]
-            packet[step // parts, pl.ds(tap, 1), place] = jnp.sum(
+            packet[step // parts, pl.ds(tap, 1), there] = jnp.sum(
                 value * (masks[tap] * moved), axis=0, keepdims=True
             )
 
-
-def taps(grad, panel, standard, inv_std, gain, glu, masks, loss):
+    mine[...] = packet[place[0]]
+    sent[...] = packet[1 - place[0]].astype(BF16)
+
+
+def taps(grad, panel, standard, inv_std, gain, glu, masks, loss, core):
     rows, width = standard.shape
     whole = pl.BlockSpec(memory_space=pltpu.HBM)
+    half = ((masks.shape[0] + 9) // 8 * 8, width // 2)
     vmem = pl.BlockSpec(memory_space=pltpu.VMEM)
     return pl.pallas_call(
         taps_kernel,
         out_shape=(
-            jax.ShapeDtypeStruct((2, (masks.shape[0] + 9) // 8 * 8, width // 2), F32),
+            jax.ShapeDtypeStruct(half, F32),
+            jax.ShapeDtypeStruct(half, BF16),
             jax.ShapeDtypeStruct((rows + 2 * EDGE, width), F32),
         ),
         in_specs=[vmem, whole, whole, vmem, vmem, whole, whole]
-        + [pl.BlockSpec(memory_space=pltpu.SMEM)],
-        out_specs=(vmem, vmem),
+        + [pl.BlockSpec(memory_space=pltpu.SMEM)] * 2,
+        out_specs=(vmem,) * 3,
         scratch_shapes=[
             pltpu.VMEM((rows, width), F32),
             pltpu.VMEM((rows + 2 * EDGE, width), F32),
+            pltpu.VMEM((2, *half), F32),
             pltpu.VMEM(panel.shape, BF16),
             pltpu.VMEM(standard.shape, F32),
             pltpu.VMEM(glu.shape, BF16),
@@ -600,7 +576,7 @@
         compiler_params=pltpu.CompilerParams(vmem_limit_bytes=60 << 20),
         cost_estimate=pl.CostEstimate(flops=1000, bytes_accessed=1000, transcendentals=0),
         name="taps",
-    )(grad, panel, standard, inv_std, gain[None, :], glu, masks, loss)
+    )(grad, panel, standard, inv_std, gain[None, :], glu, masks, loss, core[None])
 
 
 def spread_kernel(conv_grad, kernel, masks, out):
@@ -727,7 +703,8 @@
         concat_axis=0,
         tiled=True,
     )
-    packet, conv_grad = taps(
+    core = d & 1
+    packet, packet_sent, conv_grad = taps(
         grad_residual,
         full_panel,
         standard,
@@ -736,15 +713,14 @@
         glu_owned,
         masks,
         loss_part.reshape(1, 1),
-    )
-
-    core = d & 1
-    packet = after(packet, cols)
-    packet = pick(packet, core) + flip_dp(pick(packet, 1 - core).astype(BF16), 1).astype(F32)
+        core,
+    )
+
+    packet = packet + flip_dp(after(packet_sent, cols), 1).astype(F32)
     packet = packet.astype(BF16)
     cols = after(cols, packet)
-    point_own, point_sent = point_part(cols, [acts[mask] for mask in range(n_dp)], d, f)
-    sides = [(keep, after(other, point_sent), left) for keep, other, left in sides]
+    point_own, *point_sent = point_part(cols, [acts[mask] for mask in range(n_dp)], d, f)
+    sides = [(keep, after(other, *point_sent), left) for keep, other, left in sides]
     sides = middle_folds(sides, d)
     ready = [keep for keep, _, _ in sides]
     others = [after(flip_dp(packet, mask), *ready) for mask in range(2, n_dp, 2)]
@@ -752,10 +728,13 @@
     packet = packet.astype(BF16)
     grad_point = tree_sum(
         [point_own]
-        + [flip_fsdp(point_sent[mask], mask).astype(F32) for mask in range(1, n_fsdp)]
+        + [
+            flip_fsdp(after(sent, packet), mask + 1).astype(F32)
+            for mask, sent in enumerate(point_sent)
+        ]
     ).T
     grad_glu = spread(after(conv_grad, packet), conv_kernel, masks)
-    grad_head = last_fold([after(part, packet) for keep, other, _ in sides for part in (keep, other)])
+    grad_head = last_fold([after(part, packet, grad_point) for keep, other, _ in sides for part in (keep, other)])
     others = [
         after(flip_fsdp(packet, mask), grad_glu, grad_head) for mask in range(1, n_fsdp)
     ]

time: 214 us -> 205 us (0.958)
  waiting for transfers between devices: 63 us -> 53.4 us
  Pallas kernels: 59.1 us -> 52.7 us
  local copies, waits for them, and re-layouts: 18.3 us -> 22.9 us
  matrix products: 7.37 us -> 11 us
    pallas_call x3 -> x2, Pallas kernels: 24.8 us -> 16.7 us  [the longest x1 11.4 us: taps(): pl.pallas_call(taps_kernel, out_shape=(jax.ShapeDtypeStruct(half, F32), j...]
    unnamed x70 -> x96, local copies, waits for them, and re-layouts: 5.24 us -> 10 us
    ppermute x1, waiting for transfers between devices: 3.91 us -> 0.03 us  [scatter_rows(): across = lax.ppermute(block, 'fsdp', [(2, 0), (1, 3), (3, 2), (0, 1)])]
    dot_general x0 -> x1, matrix products: none -> 3.7 us  [head_grad(): lax.dot_general(jnp.concatenate([block for _, block in gathered]), jnp.co...]
    ppermute x22, waiting for transfers between devices: 10.2 us -> 7.26 us  [flip_dp(): return lax.ppermute(value, 'dp', [(i, i ^ mask) for i in range(count)])]
    ppermute x9, starting transfers between devices: 13.2 us -> 10.8 us  [flip_fsdp(): return lax.ppermute(value, 'fsdp', [(i, i ^ mask) for i in range(count)])]
  transfers between devices with their start and end apart: 42 -> 42, of which waited for: 17 -> 18; matrix products, arithmetic and copies ran while one was open for 10% -> 11% of each run, Pallas kernels for 19% -> 21%
where the time goes in v1:
time: 205 us; the launch traced here: 204 us
  waiting for transfers between devices  53.4 us (26%)
  Pallas kernels  52.7 us (26%)
  starting transfers between devices  50 us (24%)
  local copies, waits for them, and re-layouts  22.9 us (11%)
  other arithmetic  11.1 us (5%)
  matrix products  11 us (5%)
  between operations  3.2 us (2%)
    ppermute x7, waiting for transfers between devices, shift_fsdp(): lax.ppermute(value, 'fsdp', [(i, (i + step) % count) for i in range(count)])  28.1 us
    ppermute x22, starting transfers between devices, flip_dp(): return lax.ppermute(value, 'dp', [(i, i ^ mask) for i in range(count)])  16.4 us
    ppermute x7, starting transfers between devices, shift_fsdp(): lax.ppermute(value, 'fsdp', [(i, (i + step) % count) for i in range(count)])  14.7 us
    pallas_call x1, Pallas kernels, taps(): pl.pallas_call(taps_kernel, out_shape=(jax.ShapeDtypeStruct(half, F32), j...  11.4 us
    ppermute x9, starting transfers between devices, flip_fsdp(): return lax.ppermute(value, 'fsdp', [(i, i ^ mask) for i in range(count)])  10.8 us
    unnamed x96, local copies, waits for them, and re-layouts  10 us
    pallas_call x2, Pallas kernels, code_grad(): pl.pallas_call(functools.partial(code_kernel, count), out_shape=[jax.Shap...  9.17 us
    ppermute x9, waiting for transfers between devices, flip_fsdp(): return lax.ppermute(value, 'fsdp', [(i, i ^ mask) for i in range(count)])  8.55 us
  transfers between devices with their start and end apart: 42, of which 18 were waited for; matrix products, arithmetic and copies ran while one was open for 11% of the time, Pallas kernels for 21%

profile of v1, /device:TPU:0, one launch (start us, length us, event | category | flops | bytes accessed | tf_op | source)
XLA Modules:
  0.0 204.3 jit_solution(17947989154748956487)
XLA Ops:
  2.9 3.0 %collective-permute-start = (bf16[2,48,1536]{2,1,0:T(8,128)(2,1)}, bf16[2,48,1536]{2,1,0:T(8,128)(2,1)S(1)}, u32[]{:S(2)}, u32[]{:S(2)}) collective-permute-start(bf16[2,48,1536]{2,1,0:T(8,128)(2,1)} %pad_maximum_fusion.2), channel_id=1, source_target_pairs={{0,1},{1,2},{2,3},{3,0},{4,5},{5,6},{6,7},{7,4},{8,9},{9,10},{10,1... | collective-permute-start | bytes 884744 | tf_op jit(solution)/shard_map/ppermute | solution.py:26
  5.9 2.6 %collective-permute-start.1 = (bf16[2,48,1536]{2,1,0:T(8,128)(2,1)}, bf16[2,48,1536]{2,1,0:T(8,128)(2,1)}, u32[]{:S(2)}, u32[]{:S(2)}) collective-permute-start(bf16[2,48,1536]{2,1,0:T(8,128)(2,1)} %pad_maximum_fusion.2), channel_id=1, source_target_pairs={{0,2},{1,3},{2,0},{3,1},{4,6},{5,7},{6,4},{7,5},{8,10},{9,11},{10,... | collective-permute-start | bytes 884744 | tf_op jit(solution)/shard_map/ppermute | solution.py:26
  13.8 3.9 %all-to-all-start = ((bf16[8,64,1536]{2,1,0:T(8,128)(2,1)}), bf16[8,64,1536]{2,1,0:T(8,128)(2,1)S(1)}, u32[]{:S(2)}, u32[]{:S(2)}) async-start(bf16[8,64,1536]{2,1,0:T(8,128)(2,1)} %pad_maximum_fusion), calls=%async_computation | async-start | bytes 3145728 | tf_op jit(solution)/shard_map/all_to_all | solution.py:635
  17.7 10.3 %collective-permute-done.1 = bf16[2,48,1536]{2,1,0:T(8,128)(2,1)} collective-permute-done((bf16[2,48,1536]{2,1,0:T(8,128)(2,1)}, bf16[2,48,1536]{2,1,0:T(8,128)(2,1)}, u32[]{:S(2)}, u32[]{:S(2)}) %collective-permute-start.1) | collective-permute-done | bytes 294944 | tf_op jit(solution)/shard_map/ppermute | solution.py:26
  35.0 4.2 %all-to-all-done.sent = bf16[8,64,1536]{2,1,0:T(8,128)(2,1)S(1)} async-done(((bf16[8,64,1536]{2,1,0:T(8,128)(2,1)}), bf16[8,64,1536]{2,1,0:T(8,128)(2,1)S(1)}, u32[]{:S(2)}, u32[]{:S(2)}) %all-to-all-start) | async-done | bytes 1572896 | tf_op jit(solution)/shard_map/all_to_all | solution.py:635
  41.1 8.2 %forward.1 = (bf16[128,1536]{1,0:T(8,128)(2,1)}, bf16[128,1536]{1,0:T(8,128)(2,1)}, f32[128,1536]{1,0:T(8,128)}, f32[128,1]{1,0:T(8,128)}, bf16[128,1536]{1,0:T(8,128)(2,1)}) custom-call(bf16[8,64,1536]{2,1,0:T(8,128)(2,1)} %copy-done.14, s32[128,1]{1,0:T(8,128)} %copy.22.slots, f32[31,128,128]{2,1,0:T(8,128)} %broadcast_in_dim.79.masks, f32[31,1536]{1,0:T(8,128)} %kernel.3, ...), custom_call_target="tpu_custom_call" | custom-call | flops 1000000000 | bytes 6000000 | tf_op jit(solution)/shard_map/forward/pallas_call | solution.py:189
  52.8 6.5 %branch.1 = (bf16[4,2,2,2,48,1536]{5,4,3,2,1,0:T(8,128)(2,1)}, bf16[128,1536]{1,0:T(8,128)(2,1)}) custom-call(s32[2]{0:T(128)} %pad_add_fusion.1.place, bf16[2,2,2,48,1536]{4,3,2,1,0:T(8,128)(2,1)} %bitcast.229, bf16[128,1536]{1,0:T(8,128)(2,1)} %get-tuple-element.72.act.refs_0_, bf16[128,1536]{1,0:T(8,128)(2,1)} %get-tuple-element.68.residual, ...), custom_call_target="tpu_custom_call" | custom-call | tf_op jit(solution)/shard_map/branch/pallas_call | solution.py:106
  59.4 2.7 %collective-permute-start.8 = (bf16[128,1536]{1,0:T(8,128)(2,1)}, bf16[128,1536]{1,0:T(8,128)(2,1)S(1)}, u32[]{:S(2)}, u32[]{:S(2)}) collective-permute-start(bf16[128,1536]{1,0:T(8,128)(2,1)} %get-tuple-element.71), channel_id=1, source_target_pairs={{0,1},{1,2},{2,3},{3,0},{4,5},{5,6},{6,7},{7,4},{8,9},{9,10},{10,1... | collective-permute-start | bytes 1179656 | tf_op jit(solution)/shard_map/ppermute | solution.py:26
  66.7 4.0 %fusion.45 = (f32[128]{0:T(128)S(1)}, f32[128,2048]{1,0:T(8,128)S(1)}) fusion(bf16[128,1536]{1,0:T(8,128)(2,1)} %get-tuple-element.71, bf16[1536,2048]{1,0:T(8,128)(2,1)} %refs_1_.1), kind=kOutput, calls=%fused_computation.167 | convolution fusion | flops 805568384 | bytes 7733760 | tf_op jit(solution)/shard_map/dot_general | solution.py:661
  73.4 7.7 %collective-permute-done.9 = bf16[128,1536]{1,0:T(8,128)(2,1)S(1)} collective-permute-done((bf16[128,1536]{1,0:T(8,128)(2,1)}, bf16[128,1536]{1,0:T(8,128)(2,1)S(1)}, u32[]{:S(2)}, u32[]{:S(2)}) %collective-permute-start.9) | collective-permute-done | bytes 393248 | tf_op jit(solution)/shard_map/ppermute | solution.py:26
  87.2 5.3 %collective-permute-done.10 = bf16[128,1536]{1,0:T(8,128)(2,1)S(1)} collective-permute-done((bf16[128,1536]{1,0:T(8,128)(2,1)S(1)}, bf16[128,1536]{1,0:T(8,128)(2,1)S(1)}, u32[]{:S(2)}, u32[]{:S(2)}) %collective-permute-start.10) | collective-permute-done | bytes 393248 | tf_op jit(solution)/shard_map/ppermute | solution.py:334
  102.5 4.2 %code.3 = (bf16[128,2048]{1,0:T(8,128)(2,1)S(1)}, bf16[128,1536]{1,0:T(8,128)(2,1)}) custom-call(s32[1]{0:T(128)} %bitcast.77.index, f32[4,128]{1,0:T(4,128)S(1)} %get-tuple-element.136.norms, f32[4,128]{1,0:T(4,128)S(1)} %convert_element_type.76.targets, f32[128,2048]{1,0:T(8,128)S(1)} %get-tuple-element.178.refs_0_, bf16[1536,2048]{1,0:T(8,128)(2,1)S(1)} %bitcast.218), custom_call_target="tpu_custom_call" | custom-call | flops 800000000 | bytes 8000000 | tf_op jit(solution)/shard_map/code/pallas_call | solution.py:257
  106.9 2.8 %copy-done.2 = bf16[1536,2048]{1,0:T(8,128)(2,1)S(1)} copy-done((bf16[1536,2048]{1,0:T(8,128)(2,1)S(1)}, bf16[1536,2048]{1,0:T(8,128)(2,1)}, u32[]{:S(2)}) %copy-start.2) | copy-done | bytes 6291480
  110.9 4.9 %code.2 = (bf16[128,2048]{1,0:T(8,128)(2,1)S(1)}, bf16[128,2048]{1,0:T(8,128)(2,1)S(1)}, bf16[128,2048]{1,0:T(8,128)(2,1)S(1)}, f32[128,1536]{1,0:T(8,128)S(1)},...) custom-call(s32[3]{0:T(128)S(1)} %pad_add_fusion.index, f32[4,128]{1,0:T(4,128)S(1)} %get-tuple-element.136.norms, ...), custom_call_target="tpu_custom_call" | custom-call | flops 2400000000 | bytes 8000000 | tf_op jit(solution)/shard_map/code/pallas_call | solution.py:257
  117.4 3.7 %convolution_convert_fusion = bf16[1536,2048]{1,0:T(8,128)(2,1)S(1)} fusion(bf16[128,2048]{1,0:T(8,128)(2,1)S(1)} %get-tuple-element.86, bf16[128,2048]{1,0:T(8,128)(2,1)S(1)} %get-tuple-element.84, bf16[128,2048]{1,0:T(8,128)(2,1)S(1)} %get-tuple-element.82, bf16[128,2048]{1,0:T(8,128)(2,1)S(1)} %get-tuple-element.80, bf16[128,1536]{1,0:T(8,128)(2,1)S(1)} %copy-done.25, ...), kind=kOutput, calls=%fused_computation.2 | convolution fusion | flops 3239051264 | bytes 9961472 | tf_op jit(solution)/shard_map/dot_general | solution.py:344
  124.6 2.5 %collective-permute-start.22 = (bf16[128,1536]{1,0:T(8,128)(2,1)S(1)}, bf16[128,1536]{1,0:T(8,128)(2,1)S(1)}, u32[]{:S(2)}, u32[]{:S(2)}) collective-permute-start(bf16[128,1536]{1,0:T(8,128)(2,1)S(1)} %get-tuple-element.141), channel_id=1, source_target_pairs={{0,1},{1,2},{2,3},{3,0},{4,5},{5,6},{6,7},{7,4},{8,9},{9,10},{10,1... | collective-permute-start | bytes 1179656 | tf_op jit(solution)/shard_map/ppermute | solution.py:26
  130.6 2.8 %copy-done.4 = bf16[1536,2048]{1,0:T(8,128)(2,1)S(1)} copy-done((bf16[1536,2048]{1,0:T(8,128)(2,1)S(1)}, bf16[1536,2048]{1,0:T(8,128)(2,1)}, u32[]{:S(2)}) %copy-start.4) | copy-done | bytes 6291480
  133.4 4.0 %fold.2 = (bf16[2,1,192,1024]{3,2,1,0:T(8,128)(2,1)S(1)}, bf16[2,1,192,1024]{3,2,1,0:T(8,128)(2,1)}, bf16[1,2,192,1024]{3,2,1,0:T(8,128)(2,1)S(1)}, bf16[1,2,192,1024]{3,2,1,0:T(8,128)(2,1)}) custom-call(s32[3]{0:T(128)S(1)} %add_add_fusion.2.place, bf16[2,2,1,2,192,2048]{5,4,3,2,1,0:T(8,128)(2,1)S(1)} %bitcast.220, ...), custom_call_target="tpu_custom_call" | custom-call | flops 1000 | bytes 1000 | tf_op jit(solution)/shard_map/fold/pallas_call | solution.py:412
  139.4 7.0 %collective-permute-done.24 = bf16[128,1536]{1,0:T(8,128)(2,1)S(1)} collective-permute-done((bf16[128,1536]{1,0:T(8,128)(2,1)S(1)}, bf16[128,1536]{1,0:T(8,128)(2,1)S(1)}, u32[]{:S(2)}, u32[]{:S(2)}) %collective-permute-start.24) | collective-permute-done | bytes 393248 | tf_op jit(solution)/shard_map/ppermute | solution.py:26
  148.6 3.5 %all-to-all-start.1 = ((bf16[8,192,128]{2,1,0:T(8,128)(2,1)}), bf16[8,192,128]{2,1,0:T(8,128)(2,1)S(1)}, u32[]{:S(2)}, u32[]{:S(2)}) async-start(bf16[8,192,128]{2,1,0:T(8,128)(2,1)} %bitcast.91), calls=%async_computation.1 | async-start | bytes 786432 | tf_op jit(solution)/shard_map/all_to_all | solution.py:699
  152.0 11.4 %taps.1 = (f32[40,768]{1,0:T(8,128)}, bf16[40,768]{1,0:T(8,128)(2,1)}, f32[160,1536]{1,0:T(8,128)}) custom-call(bf16[128,1536]{1,0:T(8,128)(2,1)} %copy-done.15, bf16[1536,1536]{1,0:T(8,128)(2,1)} %bitcast.228, f32[128,1536]{1,0:T(8,128)} %get-tuple-element.92.standard, f32[128,1]{1,0:T(8,128)} %get-tuple-element.93.inv_std, ...), custom_call_target="tpu_custom_call" | custom-call | flops 1000 | bytes 1000 | tf_op jit(solution)/shard_map/taps/pallas_call | solution.py:556
  169.6 5.3 %point.1 = (f32[192,384]{1,0:T(8,128)}, bf16[192,384]{1,0:T(8,128)(2,1)}, bf16[192,384]{1,0:T(8,128)(2,1)}, bf16[192,384]{1,0:T(8,128)(2,1)}) custom-call(s32[2]{0:T(128)} %pad_add_fusion.1.place, bf16[8,192,128]{2,1,0:T(8,128)(2,1)} %copy-done.23, bf16[128,1536]{1,0:T(8,128)(2,1)} %get-tuple-element.72.act.refs_0_, bf16[128,1536]{1,0:T(8,128)(2,1)} %copy-done.32, ...), custom_call_target="tpu_custom_call" | custom-call | flops 1000 | bytes 1000 | tf_op jit(solution)/shard_map/point/pallas_call | solution.py:309
  185.1 4.6 %spread.1 = bf16[128,1536]{1,0:T(8,128)(2,1)} custom-call(f32[160,1536]{1,0:T(8,128)S(1)} %copy-done.11, f32[31,1536]{1,0:T(8,128)S(1)} %copy-done.10, f32[31,128,128]{2,1,0:T(8,128)S(1)} %copy-done.5), custom_call_target="tpu_custom_call" | custom-call | flops 6000000000 | bytes 3000000 | tf_op jit(solution)/shard_map/spread/pallas_call | solution.py:601
  189.7 2.6 %collective-permute-done.33 = bf16[192,384]{1,0:T(8,128)(2,1)S(1)} collective-permute-done((bf16[192,384]{1,0:T(8,128)(2,1)S(1)}, bf16[192,384]{1,0:T(8,128)(2,1)S(1)}, u32[]{:S(2)}, u32[]{:S(2)}) %collective-permute-start.33) | collective-permute-done | bytes 147488 | tf_op jit(solution)/shard_map/ppermute | solution.py:21
  (227 shorter events, 83.4 us)
Async XLA Ops:
  2.9 14.9 %collective-permute-start = (bf16[2,48,1536]{2,1,0:T(8,128)(2,1)}, bf16[2,48,1536]{2,1,0:T(8,128)(2,1)S(1)}, u32[]{:S(2)}, u32[]{:S(2)}) collective-permute-start(bf16[2,48,1536]{2,1,0:T(8,128)(2,1)} %pad_maximum_fusion.2), channel_id=1, source_target_pairs={{0,1},{1,2},{2,3},{3,0},{4,5},{5,6},{6,7},{7,4},{8,9},{9,10},{10,1... | collective-permute-start | bytes 884744 | tf_op jit(solution)/shard_map/ppermute | solution.py:26
  5.9 22.1 %collective-permute-start.1 = (bf16[2,48,1536]{2,1,0:T(8,128)(2,1)}, bf16[2,48,1536]{2,1,0:T(8,128)(2,1)}, u32[]{:S(2)}, u32[]{:S(2)}) collective-permute-start(bf16[2,48,1536]{2,1,0:T(8,128)(2,1)} %pad_maximum_fusion.2), channel_id=1, source_target_pairs={{0,2},{1,3},{2,0},{3,1},{4,6},{5,7},{6,4},{7,5},{8,10},{9,11},{10,... | collective-permute-start | bytes 884744 | tf_op jit(solution)/shard_map/ppermute | solution.py:26
  8.5 19.5 %collective-permute-start.2 = (bf16[2,48,1536]{2,1,0:T(8,128)(2,1)}, bf16[2,48,1536]{2,1,0:T(8,128)(2,1)}, u32[]{:S(2)}, u32[]{:S(2)}) collective-permute-start(bf16[2,48,1536]{2,1,0:T(8,128)(2,1)} %pad_maximum_fusion.2), channel_id=1, source_target_pairs={{0,3},{1,0},{2,1},{3,2},{4,7},{5,4},{6,5},{7,6},{8,11},{9,8},{10,9... | collective-permute-start | bytes 884744 | tf_op jit(solution)/shard_map/ppermute | solution.py:26
  13.8 25.4 %all-to-all-start = ((bf16[8,64,1536]{2,1,0:T(8,128)(2,1)}), bf16[8,64,1536]{2,1,0:T(8,128)(2,1)S(1)}, u32[]{:S(2)}, u32[]{:S(2)}) async-start(bf16[8,64,1536]{2,1,0:T(8,128)(2,1)} %pad_maximum_fusion), calls=%async_computation | async-start | bytes 3145728 | tf_op jit(solution)/shard_map/all_to_all | solution.py:635
  29.2 21.3 %collective-permute-start.5 = (bf16[2,3,48,1536]{3,2,1,0:T(8,128)(2,1)S(1)}, bf16[2,3,48,1536]{3,2,1,0:T(8,128)(2,1)}, u32[]{:S(2)}, u32[]{:S(2)}) collective-permute-start(bf16[2,3,48,1536]{3,2,1,0:T(8,128)(2,1)S(1)} %pad_maximum_fusion.1.got), channel_id=1, source_target_pairs={{0,4},{4,0},{8,12},{12,8},{16,20},{20,16},{24,28},{28,24},{1,5},{5... | collective-permute-start | bytes 2654216 | tf_op jit(solution)/shard_map/ppermute | solution.py:16
  30.4 18.9 %collective-permute-start.4 = (bf16[3,48,1536]{2,1,0:T(8,128)(2,1)}, bf16[3,48,1536]{2,1,0:T(8,128)(2,1)S(1)}, u32[]{:S(2)}, u32[]{:S(2)}) collective-permute-start(bf16[3,48,1536]{2,1,0:T(8,128)(2,1)} %get-tuple-element.139), channel_id=1, source_target_pairs={{0,16},{4,20},{8,24},{12,28},{16,0},{20,4},{24,8},{28,12},{1,17},{... | collective-permute-start | bytes 1327112 | tf_op jit(solution)/shard_map/ppermute | solution.py:16
  31.9 17.5 %collective-permute-start.3 = (bf16[3,48,1536]{2,1,0:T(8,128)(2,1)}, bf16[3,48,1536]{2,1,0:T(8,128)(2,1)}, u32[]{:S(2)}, u32[]{:S(2)}) collective-permute-start(bf16[3,48,1536]{2,1,0:T(8,128)(2,1)} %get-tuple-element.140), channel_id=1, source_target_pairs={{0,8},{4,12},{8,0},{12,4},{16,24},{20,28},{24,16},{28,20},{1,9},{5... | collective-permute-start | bytes 1327112 | tf_op jit(solution)/shard_map/ppermute | solution.py:16
  59.4 14.1 %collective-permute-start.8 = (bf16[128,1536]{1,0:T(8,128)(2,1)}, bf16[128,1536]{1,0:T(8,128)(2,1)S(1)}, u32[]{:S(2)}, u32[]{:S(2)}) collective-permute-start(bf16[128,1536]{1,0:T(8,128)(2,1)} %get-tuple-element.71), channel_id=1, source_target_pairs={{0,1},{1,2},{2,3},{3,0},{4,5},{5,6},{6,7},{7,4},{8,9},{9,10},{10,1... | collective-permute-start | bytes 1179656 | tf_op jit(solution)/shard_map/ppermute | solution.py:26
  62.0 19.1 %collective-permute-start.9 = (bf16[128,1536]{1,0:T(8,128)(2,1)}, bf16[128,1536]{1,0:T(8,128)(2,1)S(1)}, u32[]{:S(2)}, u32[]{:S(2)}) collective-permute-start(bf16[128,1536]{1,0:T(8,128)(2,1)} %get-tuple-element.71), channel_id=1, source_target_pairs={{0,3},{1,0},{2,1},{3,2},{4,7},{5,4},{6,5},{7,6},{8,11},{9,8},{10,9... | collective-permute-start | bytes 1179656 | tf_op jit(solution)/shard_map/ppermute | solution.py:26
  63.2 19.9 %collective-permute-start.11 = (bf16[128,1536]{1,0:T(8,128)(2,1)S(1)}, bf16[128,1536]{1,0:T(8,128)(2,1)S(1)}, u32[]{:S(2)}, u32[]{:S(2)}) collective-permute-start(bf16[128,1536]{1,0:T(8,128)(2,1)S(1)} %copy-done.22), channel_id=1, source_target_pairs={{0,8},{4,12},{8,0},{12,4},{16,24},{20,28},{24,16},{28,20},{1,9},{5... | collective-permute-start | bytes 1179656 | tf_op jit(solution)/shard_map/ppermute | solution.py:16
  63.7 20.0 %collective-permute-start.12 = (bf16[128,1536]{1,0:T(8,128)(2,1)S(1)}, bf16[128,1536]{1,0:T(8,128)(2,1)S(1)}, u32[]{:S(2)}, u32[]{:S(2)}) collective-permute-start(bf16[128,1536]{1,0:T(8,128)(2,1)S(1)} %copy-done.22), channel_id=1, source_target_pairs={{0,16},{4,20},{8,24},{12,28},{16,0},{20,4},{24,8},{28,12},{1,17},{... | collective-permute-start | bytes 1179656 | tf_op jit(solution)/shard_map/ppermute | solution.py:16
  64.4 21.0 %collective-permute-start.13 = (bf16[128,1536]{1,0:T(8,128)(2,1)S(1)}, bf16[128,1536]{1,0:T(8,128)(2,1)S(1)}, u32[]{:S(2)}, u32[]{:S(2)}) collective-permute-start(bf16[128,1536]{1,0:T(8,128)(2,1)S(1)} %copy-done.22), channel_id=1, source_target_pairs={{0,24},{4,28},{8,16},{12,20},{16,8},{20,12},{24,0},{28,4},{1,25},{... | collective-permute-start | bytes 1179656 | tf_op jit(solution)/shard_map/ppermute | solution.py:16
  73.4 12.5 %collective-permute-start.14 = (bf16[128,1536]{1,0:T(8,128)(2,1)S(1)}, bf16[128,1536]{1,0:T(8,128)(2,1)S(1)}, u32[]{:S(2)}, u32[]{:S(2)}) collective-permute-start(bf16[128,1536]{1,0:T(8,128)(2,1)S(1)} %copy-done.22), channel_id=1, source_target_pairs={{0,4},{4,0},{8,12},{12,8},{16,20},{20,16},{24,28},{28,24},{1,5},{5... | collective-permute-start | bytes 1179656 | tf_op jit(solution)/shard_map/ppermute | solution.py:16
  81.2 11.2 %collective-permute-start.10 = (bf16[128,1536]{1,0:T(8,128)(2,1)S(1)}, bf16[128,1536]{1,0:T(8,128)(2,1)S(1)}, u32[]{:S(2)}, u32[]{:S(2)}) collective-permute-start(bf16[128,1536]{1,0:T(8,128)(2,1)S(1)} %select_select_fusion), channel_id=1, source_target_pairs={{0,2},{3,1},{2,3},{1,0},{4,6},{7,5},{6,7},{5,4},{8,10},{11,9},{10,... | collective-permute-start | bytes 1179656 | tf_op jit(solution)/shard_map/ppermute | solution.py:334
  124.6 13.8 %collective-permute-start.22 = (bf16[128,1536]{1,0:T(8,128)(2,1)S(1)}, bf16[128,1536]{1,0:T(8,128)(2,1)S(1)}, u32[]{:S(2)}, u32[]{:S(2)}) collective-permute-start(bf16[128,1536]{1,0:T(8,128)(2,1)S(1)} %get-tuple-element.141), channel_id=1, source_target_pairs={{0,1},{1,2},{2,3},{3,0},{4,5},{5,6},{6,7},{7,4},{8,9},{9,10},{10,1... | collective-permute-start | bytes 1179656 | tf_op jit(solution)/shard_map/ppermute | solution.py:26
  127.2 19.2 %collective-permute-start.24 = (bf16[128,1536]{1,0:T(8,128)(2,1)S(1)}, bf16[128,1536]{1,0:T(8,128)(2,1)S(1)}, u32[]{:S(2)}, u32[]{:S(2)}) collective-permute-start(bf16[128,1536]{1,0:T(8,128)(2,1)S(1)} %get-tuple-element.142), channel_id=1, source_target_pairs={{0,3},{1,0},{2,1},{3,2},{4,7},{5,4},{6,5},{7,6},{8,11},{9,8},{10,9... | collective-permute-start | bytes 1179656 | tf_op jit(solution)/shard_map/ppermute | solution.py:26
  138.4 36.5 %collective-permute-start.28 = (bf16[1,2,192,1024]{3,2,1,0:T(8,128)(2,1)}, bf16[1,2,192,1024]{3,2,1,0:T(8,128)(2,1)}, u32[]{:S(2)}, u32[]{:S(2)}) collective-permute-start(bf16[1,2,192,1024]{3,2,1,0:T(8,128)(2,1)} %get-tuple-element.105), channel_id=1, source_target_pairs={{0,16},{4,20},{8,24},{12,28},{16,0},{20,4},{24,8},{28,12},{1,17},{... | collective-permute-start | bytes 2359304 | tf_op jit(solution)/shard_map/ppermute | solution.py:16
  138.9 36.0 %collective-permute-start.27 = (bf16[2,1,192,1024]{3,2,0,1:T(8,128)(2,1)}, bf16[2,1,192,1024]{3,2,0,1:T(8,128)(2,1)}, u32[]{:S(2)}, u32[]{:S(2)}) collective-permute-start(bf16[2,1,192,1024]{3,2,0,1:T(8,128)(2,1)} %bitcast.93), channel_id=1, source_target_pairs={{0,8},{4,12},{8,0},{12,4},{16,24},{20,28},{24,16},{28,20},{1,9},{5... | collective-permute-start | bytes 2359304 | tf_op jit(solution)/shard_map/ppermute | solution.py:16
  148.6 14.9 %all-to-all-start.1 = ((bf16[8,192,128]{2,1,0:T(8,128)(2,1)}), bf16[8,192,128]{2,1,0:T(8,128)(2,1)S(1)}, u32[]{:S(2)}, u32[]{:S(2)}) async-start(bf16[8,192,128]{2,1,0:T(8,128)(2,1)} %bitcast.91), calls=%async_computation.1 | async-start | bytes 786432 | tf_op jit(solution)/shard_map/all_to_all | solution.py:699
  177.2 12.5 %collective-permute-start.32 = (bf16[192,384]{1,0:T(8,128)(2,1)S(1)}, bf16[192,384]{1,0:T(8,128)(2,1)S(1)}, u32[]{:S(2)}, u32[]{:S(2)}) collective-permute-start(bf16[192,384]{1,0:T(8,128)(2,1)S(1)} %copy-done.44), channel_id=1, source_target_pairs={{0,1},{1,0},{2,3},{3,2},{4,5},{5,4},{6,7},{7,6},{8,9},{9,8},{10,11... | collective-permute-start | bytes 442376 | tf_op jit(solution)/shard_map/ppermute | solution.py:21
  179.0 13.4 %collective-permute-start.33 = (bf16[192,384]{1,0:T(8,128)(2,1)S(1)}, bf16[192,384]{1,0:T(8,128)(2,1)S(1)}, u32[]{:S(2)}, u32[]{:S(2)}) collective-permute-start(bf16[192,384]{1,0:T(8,128)(2,1)S(1)} %copy-done.43), channel_id=1, source_target_pairs={{0,2},{1,3},{2,0},{3,1},{4,6},{5,7},{6,4},{7,5},{8,10},{9,11},{10,... | collective-permute-start | bytes 442376 | tf_op jit(solution)/shard_map/ppermute | solution.py:21
  180.4 12.4 %collective-permute-start.34 = (bf16[192,384]{1,0:T(8,128)(2,1)S(1)}, bf16[192,384]{1,0:T(8,128)(2,1)S(1)}, u32[]{:S(2)}, u32[]{:S(2)}) collective-permute-start(bf16[192,384]{1,0:T(8,128)(2,1)S(1)} %copy-done.42), channel_id=1, source_target_pairs={{0,3},{1,2},{2,1},{3,0},{4,7},{5,6},{6,5},{7,4},{8,11},{9,10},{10,... | collective-permute-start | bytes 442376 | tf_op jit(solution)/shard_map/ppermute | solution.py:21
  181.7 13.4 %collective-permute-start.36 = (bf16[1,1,192,1024]{3,2,1,0:T(8,128)(2,1)S(1)}, bf16[1,1,192,1024]{3,2,1,0:T(8,128)(2,1)S(1)}, u32[]{:S(2)}, u32[]{:S(2)}) collective-permute-start(bf16[1,1,192,1024]{3,2,1,0:T(8,128)(2,1)S(1)} %get-tuple-element.122), channel_id=1, source_target_pairs={{0,8},{4,12},{8,0},{12,4},{16,24},{20,28},{24,16},{28,20},{1,9},{5... | collective-permute-start | bytes 1179656 | tf_op jit(solution)/shard_map/ppermute | solution.py:16
  183.6 11.5 %collective-permute-start.35 = (bf16[1,1,192,1024]{3,2,1,0:T(8,128)(2,1)S(1)}, bf16[1,1,192,1024]{3,2,1,0:T(8,128)(2,1)S(1)}, u32[]{:S(2)}, u32[]{:S(2)}) collective-permute-start(bf16[1,1,192,1024]{3,2,1,0:T(8,128)(2,1)S(1)} %get-tuple-element.119), channel_id=1, source_target_pairs={{0,16},{4,20},{8,24},{12,28},{16,0},{20,4},{24,8},{28,12},{1,17},{... | collective-permute-start | bytes 1179656 | tf_op jit(solution)/shard_map/ppermute | solution.py:16
  (65 other events, 465.4 us)

commit v2 on v1

--- a/solution.py
+++ b/solution.py
@@ -352,19 +352,20 @@
         grads, outs = code_part(places, F32)
         grads, outs = dict(zip(places, grads)), dict(zip(places, outs))
         got = [shift_fsdp(outs[step].astype(BF16), step).astype(F32) for step in range(1, count)]
-        return sum(got, outs[0]), join_cores(head_grad(grads), d)
+        return sum(got, outs[0]), join_cores(head_grad(grads), None, d)
     grads = {}
     (grads[2],), (block,) = code_part([2], BF16)
     across = lax.ppermute(block, "fsdp", [(2, 0), (1, 3), (3, 2), (0, 1)])
     (grads[1], grads[3], grads[0]), (ahead, behind, own) = code_part([1, 3, 0], F32)
-    across = after(across, own).astype(F32)
+    head = head_grad(grads)
+    sent = other_core(head, d)
+    across = after(across, own, sent).astype(F32)
     ahead = (ahead + jnp.where(f == 1, across, 0.0)).astype(BF16)
     behind = (behind + jnp.where(f == 2, across, 0.0)).astype(BF16)
     got1 = shift_fsdp(ahead, 1)
     got2 = shift_fsdp(behind, -1)
     direct = jnp.where((f == 0) | (f == 3), across, 0.0)
-    head = head_grad({place: after(grads[place], ahead, behind) for place in places})
-    sides = join_cores(head, d)
+    sides = join_cores(head, after(sent, ahead, behind), d)
     got1 = after(got1, *[keep for keep, _, _ in sides])
     return own + direct + got1.astype(F32) + got2.astype(F32), sides
 
@@ -449,11 +450,20 @@
     return [list(range(1, bits))[step], list(range(bits - 1, 0, -1))[step]]
 
 
-def join_cores(head, d):
+def by_core(head):
+    count = lax.axis_size("dp")
+    return head.reshape(count // 2, 2, head.shape[0] // count, head.shape[1])
+
+
+def other_core(head, d):
+    return pick(by_core(head), 1 - (d & 1), 1)
+
+
+def join_cores(head, sent, d):
     count = lax.axis_size("dp")
     left = list(range(count.bit_length() - 2, 0, -1))
-    cut = head.reshape(count // 2, 2, head.shape[0] // count, head.shape[1])
-    got = flip_dp(pick(cut, 1 - (d & 1), 1), 1)
+    cut = by_core(head)
+    got = flip_dp(other_core(head, d) if sent is None else sent, 1)
     sides = [(cut, got, left, bit) for bit in halve_bits(0)]
     return send_on(fold(sides, d, True), 0)
 

time: 205 us -> 209 us (1.020)
  local copies, waits for them, and re-layouts: 22.9 us -> 27.5 us
  waiting for transfers between devices: 53.4 us -> 56 us
    unnamed x96 -> x100, local copies, waits for them, and re-layouts: 10 us -> 14.7 us
  transfers between devices with their start and end apart: 42 -> 42, of which waited for: 18 -> 20; matrix products, arithmetic and copies ran while one was open for 11% -> 13% of each run, Pallas kernels for 21% -> 18%
where the time goes in v2:
time: 209 us; the launch traced here: 208 us
  waiting for transfers between devices  56 us (27%)
  Pallas kernels  52.1 us (25%)
  starting transfers between devices  48.3 us (23%)
  local copies, waits for them, and re-layouts  27.5 us (13%)
  matrix products  11 us (5%)
  other arithmetic  9.63 us (5%)
  between operations  3.19 us (2%)
    ppermute x7, waiting for transfers between devices, shift_fsdp(): lax.ppermute(value, 'fsdp', [(i, (i + step) % count) for i in range(count)])  27.1 us
    unnamed x100, local copies, waits for them, and re-layouts  14.7 us
    ppermute x7, starting transfers between devices, shift_fsdp(): lax.ppermute(value, 'fsdp', [(i, (i + step) % count) for i in range(count)])  14.7 us
    ppermute x22, starting transfers between devices, flip_dp(): return lax.ppermute(value, 'dp', [(i, i ^ mask) for i in range(count)])  14.6 us
    pallas_call x1, Pallas kernels, taps(): pl.pallas_call(taps_kernel, out_shape=(jax.ShapeDtypeStruct(half, F32), j...  11.5 us
    ppermute x9, starting transfers between devices, flip_fsdp(): return lax.ppermute(value, 'fsdp', [(i, i ^ mask) for i in range(count)])  10.9 us
    ppermute x9, waiting for transfers between devices, flip_fsdp(): return lax.ppermute(value, 'fsdp', [(i, i ^ mask) for i in range(count)])  8.88 us
    pallas_call x2, Pallas kernels, code_grad(): pl.pallas_call(functools.partial(code_kernel, count), out_shape=[jax.Shap...  8.42 us
  transfers between devices with their start and end apart: 42, of which 20 were waited for; matrix products, arithmetic and copies ran while one was open for 13% of the time, Pallas kernels for 18%

profile of v2, /device:TPU:0, one launch (start us, length us, event | category | flops | bytes accessed | tf_op | source)
XLA Modules:
  0.0 207.7 jit_solution(16309011832448269098)
XLA Ops:
  2.9 3.0 %collective-permute-start = (bf16[2,48,1536]{2,1,0:T(8,128)(2,1)}, bf16[2,48,1536]{2,1,0:T(8,128)(2,1)S(1)}, u32[]{:S(2)}, u32[]{:S(2)}) collective-permute-start(bf16[2,48,1536]{2,1,0:T(8,128)(2,1)} %pad_maximum_fusion.2), channel_id=1, source_target_pairs={{0,1},{1,2},{2,3},{3,0},{4,5},{5,6},{6,7},{7,4},{8,9},{9,10},{10,1... | collective-permute-start | bytes 884744 | tf_op jit(solution)/shard_map/ppermute | solution.py:26
  13.8 3.9 %all-to-all-start = ((bf16[8,64,1536]{2,1,0:T(8,128)(2,1)}), bf16[8,64,1536]{2,1,0:T(8,128)(2,1)S(1)}, u32[]{:S(2)}, u32[]{:S(2)}) async-start(bf16[8,64,1536]{2,1,0:T(8,128)(2,1)} %pad_maximum_fusion), calls=%async_computation | async-start | bytes 3145728 | tf_op jit(solution)/shard_map/all_to_all | solution.py:645
  17.7 10.3 %collective-permute-done.1 = bf16[2,48,1536]{2,1,0:T(8,128)(2,1)} collective-permute-done((bf16[2,48,1536]{2,1,0:T(8,128)(2,1)}, bf16[2,48,1536]{2,1,0:T(8,128)(2,1)}, u32[]{:S(2)}, u32[]{:S(2)}) %collective-permute-start.1) | collective-permute-done | bytes 294944 | tf_op jit(solution)/shard_map/ppermute | solution.py:26
  35.0 4.2 %all-to-all-done.sent = bf16[8,64,1536]{2,1,0:T(8,128)(2,1)S(1)} async-done(((bf16[8,64,1536]{2,1,0:T(8,128)(2,1)}), bf16[8,64,1536]{2,1,0:T(8,128)(2,1)S(1)}, u32[]{:S(2)}, u32[]{:S(2)}) %all-to-all-start) | async-done | bytes 1572896 | tf_op jit(solution)/shard_map/all_to_all | solution.py:645
  41.1 8.2 %forward.1 = (bf16[128,1536]{1,0:T(8,128)(2,1)}, bf16[128,1536]{1,0:T(8,128)(2,1)}, f32[128,1536]{1,0:T(8,128)}, f32[128,1]{1,0:T(8,128)}, bf16[128,1536]{1,0:T(8,128)(2,1)}) custom-call(bf16[8,64,1536]{2,1,0:T(8,128)(2,1)} %copy-done.17, s32[128,1]{1,0:T(8,128)} %copy.22.slots, f32[31,128,128]{2,1,0:T(8,128)} %broadcast_in_dim.79.masks, f32[31,1536]{1,0:T(8,128)} %kernel.3, ...), custom_call_target="tpu_custom_call" | custom-call | flops 1000000000 | bytes 6000000 | tf_op jit(solution)/shard_map/forward/pallas_call | solution.py:189
  52.8 6.6 %branch.1 = (bf16[4,2,2,2,48,1536]{5,4,3,2,1,0:T(8,128)(2,1)}, bf16[128,1536]{1,0:T(8,128)(2,1)}) custom-call(s32[2]{0:T(128)} %pad_add_fusion.1.place, bf16[2,2,2,48,1536]{4,3,2,1,0:T(8,128)(2,1)} %bitcast.229, bf16[128,1536]{1,0:T(8,128)(2,1)} %get-tuple-element.69.act.refs_0_, bf16[128,1536]{1,0:T(8,128)(2,1)} %get-tuple-element.65.residual, ...), custom_call_target="tpu_custom_call" | custom-call | tf_op jit(solution)/shard_map/branch/pallas_call | solution.py:106
  59.4 2.7 %collective-permute-start.8 = (bf16[128,1536]{1,0:T(8,128)(2,1)}, bf16[128,1536]{1,0:T(8,128)(2,1)S(1)}, u32[]{:S(2)}, u32[]{:S(2)}) collective-permute-start(bf16[128,1536]{1,0:T(8,128)(2,1)} %get-tuple-element.68), channel_id=1, source_target_pairs={{0,1},{1,2},{2,3},{3,0},{4,5},{5,6},{6,7},{7,4},{8,9},{9,10},{10,1... | collective-permute-start | bytes 1179656 | tf_op jit(solution)/shard_map/ppermute | solution.py:26
  66.7 4.0 %fusion.45 = (f32[128]{0:T(128)S(1)}, f32[128,2048]{1,0:T(8,128)S(1)}) fusion(bf16[128,1536]{1,0:T(8,128)(2,1)} %get-tuple-element.68, bf16[1536,2048]{1,0:T(8,128)(2,1)} %refs_1_.1), kind=kOutput, calls=%fused_computation.167 | convolution fusion | flops 805568384 | bytes 7733760 | tf_op jit(solution)/shard_map/dot_general | solution.py:671
  73.4 7.7 %collective-permute-done.9 = bf16[128,1536]{1,0:T(8,128)(2,1)S(1)} collective-permute-done((bf16[128,1536]{1,0:T(8,128)(2,1)}, bf16[128,1536]{1,0:T(8,128)(2,1)S(1)}, u32[]{:S(2)}, u32[]{:S(2)}) %collective-permute-start.9) | collective-permute-done | bytes 393248 | tf_op jit(solution)/shard_map/ppermute | solution.py:26
  87.2 5.2 %collective-permute-done.10 = bf16[128,1536]{1,0:T(8,128)(2,1)S(1)} collective-permute-done((bf16[128,1536]{1,0:T(8,128)(2,1)S(1)}, bf16[128,1536]{1,0:T(8,128)(2,1)S(1)}, u32[]{:S(2)}, u32[]{:S(2)}) %collective-permute-start.10) | collective-permute-done | bytes 393248 | tf_op jit(solution)/shard_map/ppermute | solution.py:334
  103.6 2.8 %copy-done.2 = bf16[1536,2048]{1,0:T(8,128)(2,1)S(1)} copy-done((bf16[1536,2048]{1,0:T(8,128)(2,1)S(1)}, bf16[1536,2048]{1,0:T(8,128)(2,1)}, u32[]{:S(2)}) %copy-start.2) | copy-done | bytes 6291480
  107.6 3.5 %code.3 = (bf16[128,2048]{1,0:T(8,128)(2,1)S(1)}, bf16[128,1536]{1,0:T(8,128)(2,1)S(1)}) custom-call(s32[1]{0:T(128)} %bitcast.77.index, f32[4,128]{1,0:T(4,128)S(1)} %get-tuple-element.130.norms, f32[4,128]{1,0:T(4,128)S(1)} %convert_element_type.76.targets, f32[128,2048]{1,0:T(8,128)S(1)} %copy-done.10, bf16[1536,2048]{1,0:T(8,128)(2,1)S(1)} %copy-done.2), custom_call_target="tpu_custom_call" | custom-call | flops 800000000 | bytes 8000000 | tf_op jit(solution)/shard_map/code/pallas_call | solution.py:257
  111.1 2.8 %copy-done.3 = bf16[1536,2048]{1,0:T(8,128)(2,1)S(1)} copy-done((bf16[1536,2048]{1,0:T(8,128)(2,1)S(1)}, bf16[1536,2048]{1,0:T(8,128)(2,1)}, u32[]{:S(2)}) %copy-start.3) | copy-done | bytes 6291480
  113.9 4.9 %code.2 = (bf16[128,2048]{1,0:T(8,128)(2,1)S(1)}, bf16[128,2048]{1,0:T(8,128)(2,1)S(1)}, bf16[128,2048]{1,0:T(8,128)(2,1)S(1)}, f32[128,1536]{1,0:T(8,128)S(1)},...) custom-call(s32[3]{0:T(128)S(1)} %pad_add_fusion.index, f32[4,128]{1,0:T(4,128)S(1)} %get-tuple-element.130.norms, ...), custom_call_target="tpu_custom_call" | custom-call | flops 2400000000 | bytes 8000000 | tf_op jit(solution)/shard_map/code/pallas_call | solution.py:257
  119.7 3.7 %convolution_convert_fusion = bf16[1536,2048]{1,0:T(8,128)(2,1)S(1)} fusion(bf16[128,2048]{1,0:T(8,128)(2,1)S(1)} %get-tuple-element.76, bf16[128,2048]{1,0:T(8,128)(2,1)S(1)} %get-tuple-element.75, bf16[128,2048]{1,0:T(8,128)(2,1)S(1)} %get-tuple-element.74, bf16[128,2048]{1,0:T(8,128)(2,1)S(1)} %get-tuple-element.73, bf16[128,1536]{1,0:T(8,128)(2,1)S(1)} %copy-done.27, ...), kind=kOutput, calls=%fused_computation.2 | convolution fusion | flops 3239051264 | bytes 9961472 | tf_op jit(solution)/shard_map/dot_general | solution.py:344
  130.5 2.7 %collective-permute-start.24 = (bf16[128,1536]{1,0:T(8,128)(2,1)S(1)}, bf16[128,1536]{1,0:T(8,128)(2,1)S(1)}, u32[]{:S(2)}, u32[]{:S(2)}) collective-permute-start(bf16[128,1536]{1,0:T(8,128)(2,1)S(1)} %get-tuple-element.136), channel_id=1, source_target_pairs={{0,3},{1,0},{2,1},{3,2},{4,7},{5,4},{6,5},{7,6},{8,11},{9,8},{10,9... | collective-permute-start | bytes 1179656 | tf_op jit(solution)/shard_map/ppermute | solution.py:26
  135.4 2.8 %copy-done.5 = bf16[1536,2048]{1,0:T(8,128)(2,1)S(1)} copy-done((bf16[1536,2048]{1,0:T(8,128)(2,1)S(1)}, bf16[1536,2048]{1,0:T(8,128)(2,1)}, u32[]{:S(2)}) %copy-start.5) | copy-done | bytes 6291480
  138.2 4.0 %fold.2 = (bf16[2,1,192,1024]{3,2,1,0:T(8,128)(2,1)S(1)}, bf16[2,1,192,1024]{3,2,1,0:T(8,128)(2,1)}, bf16[1,2,192,1024]{3,2,1,0:T(8,128)(2,1)S(1)}, bf16[1,2,192,1024]{3,2,1,0:T(8,128)(2,1)}) custom-call(s32[3]{0:T(128)S(1)} %add_add_fusion.2.place, bf16[2,2,1,2,192,2048]{5,4,3,2,1,0:T(8,128)(2,1)S(1)} %bitcast.220, ...), custom_call_target="tpu_custom_call" | custom-call | flops 1000 | bytes 1000 | tf_op jit(solution)/shard_map/fold/pallas_call | solution.py:413
  144.4 5.7 %collective-permute-done.24 = bf16[128,1536]{1,0:T(8,128)(2,1)S(1)} collective-permute-done((bf16[128,1536]{1,0:T(8,128)(2,1)S(1)}, bf16[128,1536]{1,0:T(8,128)(2,1)S(1)}, u32[]{:S(2)}, u32[]{:S(2)}) %collective-permute-start.24) | collective-permute-done | bytes 393248 | tf_op jit(solution)/shard_map/ppermute | solution.py:26
  151.3 3.5 %all-to-all-start.1 = ((bf16[8,192,128]{2,1,0:T(8,128)(2,1)}), bf16[8,192,128]{2,1,0:T(8,128)(2,1)S(1)}, u32[]{:S(2)}, u32[]{:S(2)}) async-start(bf16[8,192,128]{2,1,0:T(8,128)(2,1)} %bitcast.91), calls=%async_computation.1 | async-start | bytes 786432 | tf_op jit(solution)/shard_map/all_to_all | solution.py:709
  154.8 11.5 %taps.1 = (f32[40,768]{1,0:T(8,128)}, bf16[40,768]{1,0:T(8,128)(2,1)}, f32[160,1536]{1,0:T(8,128)}) custom-call(bf16[128,1536]{1,0:T(8,128)(2,1)} %copy-done.18, bf16[1536,1536]{1,0:T(8,128)(2,1)} %bitcast.228, f32[128,1536]{1,0:T(8,128)} %get-tuple-element.86.standard, f32[128,1]{1,0:T(8,128)} %get-tuple-element.87.inv_std, ...), custom_call_target="tpu_custom_call" | custom-call | flops 1000 | bytes 1000 | tf_op jit(solution)/shard_map/taps/pallas_call | solution.py:566
  173.8 5.3 %point.1 = (f32[192,384]{1,0:T(8,128)}, bf16[192,384]{1,0:T(8,128)(2,1)}, bf16[192,384]{1,0:T(8,128)(2,1)}, bf16[192,384]{1,0:T(8,128)(2,1)}) custom-call(s32[2]{0:T(128)} %pad_add_fusion.1.place, bf16[8,192,128]{2,1,0:T(8,128)(2,1)} %copy-done.25, bf16[128,1536]{1,0:T(8,128)(2,1)} %get-tuple-element.69.act.refs_0_, bf16[128,1536]{1,0:T(8,128)(2,1)} %copy-done.34, ...), custom_call_target="tpu_custom_call" | custom-call | flops 1000 | bytes 1000 | tf_op jit(solution)/shard_map/point/pallas_call | solution.py:309
  187.9 4.6 %spread.1 = bf16[128,1536]{1,0:T(8,128)(2,1)} custom-call(f32[160,1536]{1,0:T(8,128)S(1)} %copy-done.14, f32[31,1536]{1,0:T(8,128)S(1)} %copy-done.13, f32[31,128,128]{2,1,0:T(8,128)S(1)} %copy-done.6), custom_call_target="tpu_custom_call" | custom-call | flops 6000000000 | bytes 3000000 | tf_op jit(solution)/shard_map/spread/pallas_call | solution.py:611
  192.6 3.7 %collective-permute-done.33 = bf16[192,384]{1,0:T(8,128)(2,1)S(1)} collective-permute-done((bf16[192,384]{1,0:T(8,128)(2,1)S(1)}, bf16[192,384]{1,0:T(8,128)(2,1)S(1)}, u32[]{:S(2)}, u32[]{:S(2)}) %collective-permute-start.33) | collective-permute-done | bytes 147488 | tf_op jit(solution)/shard_map/ppermute | solution.py:21
  (231 shorter events, 87.3 us)
Async XLA Ops:
  2.9 14.9 %collective-permute-start = (bf16[2,48,1536]{2,1,0:T(8,128)(2,1)}, bf16[2,48,1536]{2,1,0:T(8,128)(2,1)S(1)}, u32[]{:S(2)}, u32[]{:S(2)}) collective-permute-start(bf16[2,48,1536]{2,1,0:T(8,128)(2,1)} %pad_maximum_fusion.2), channel_id=1, source_target_pairs={{0,1},{1,2},{2,3},{3,0},{4,5},{5,6},{6,7},{7,4},{8,9},{9,10},{10,1... | collective-permute-start | bytes 884744 | tf_op jit(solution)/shard_map/ppermute | solution.py:26
  5.9 22.1 %collective-permute-start.1 = (bf16[2,48,1536]{2,1,0:T(8,128)(2,1)}, bf16[2,48,1536]{2,1,0:T(8,128)(2,1)}, u32[]{:S(2)}, u32[]{:S(2)}) collective-permute-start(bf16[2,48,1536]{2,1,0:T(8,128)(2,1)} %pad_maximum_fusion.2), channel_id=1, source_target_pairs={{0,2},{1,3},{2,0},{3,1},{4,6},{5,7},{6,4},{7,5},{8,10},{9,11},{10,... | collective-permute-start | bytes 884744 | tf_op jit(solution)/shard_map/ppermute | solution.py:26
  8.5 19.5 %collective-permute-start.2 = (bf16[2,48,1536]{2,1,0:T(8,128)(2,1)}, bf16[2,48,1536]{2,1,0:T(8,128)(2,1)}, u32[]{:S(2)}, u32[]{:S(2)}) collective-permute-start(bf16[2,48,1536]{2,1,0:T(8,128)(2,1)} %pad_maximum_fusion.2), channel_id=1, source_target_pairs={{0,3},{1,0},{2,1},{3,2},{4,7},{5,4},{6,5},{7,6},{8,11},{9,8},{10,9... | collective-permute-start | bytes 884744 | tf_op jit(solution)/shard_map/ppermute | solution.py:26
  13.8 25.4 %all-to-all-start = ((bf16[8,64,1536]{2,1,0:T(8,128)(2,1)}), bf16[8,64,1536]{2,1,0:T(8,128)(2,1)S(1)}, u32[]{:S(2)}, u32[]{:S(2)}) async-start(bf16[8,64,1536]{2,1,0:T(8,128)(2,1)} %pad_maximum_fusion), calls=%async_computation | async-start | bytes 3145728 | tf_op jit(solution)/shard_map/all_to_all | solution.py:645
  29.2 21.4 %collective-permute-start.5 = (bf16[2,3,48,1536]{3,2,1,0:T(8,128)(2,1)S(1)}, bf16[2,3,48,1536]{3,2,1,0:T(8,128)(2,1)}, u32[]{:S(2)}, u32[]{:S(2)}) collective-permute-start(bf16[2,3,48,1536]{3,2,1,0:T(8,128)(2,1)S(1)} %pad_maximum_fusion.1.got), channel_id=1, source_target_pairs={{0,4},{4,0},{8,12},{12,8},{16,20},{20,16},{24,28},{28,24},{1,5},{5... | collective-permute-start | bytes 2654216 | tf_op jit(solution)/shard_map/ppermute | solution.py:16
  30.4 18.9 %collective-permute-start.4 = (bf16[3,48,1536]{2,1,0:T(8,128)(2,1)}, bf16[3,48,1536]{2,1,0:T(8,128)(2,1)S(1)}, u32[]{:S(2)}, u32[]{:S(2)}) collective-permute-start(bf16[3,48,1536]{2,1,0:T(8,128)(2,1)} %get-tuple-element.133), channel_id=1, source_target_pairs={{0,16},{4,20},{8,24},{12,28},{16,0},{20,4},{24,8},{28,12},{1,17},{... | collective-permute-start | bytes 1327112 | tf_op jit(solution)/shard_map/ppermute | solution.py:16
  31.9 17.5 %collective-permute-start.3 = (bf16[3,48,1536]{2,1,0:T(8,128)(2,1)}, bf16[3,48,1536]{2,1,0:T(8,128)(2,1)}, u32[]{:S(2)}, u32[]{:S(2)}) collective-permute-start(bf16[3,48,1536]{2,1,0:T(8,128)(2,1)} %get-tuple-element.134), channel_id=1, source_target_pairs={{0,8},{4,12},{8,0},{12,4},{16,24},{20,28},{24,16},{28,20},{1,9},{5... | collective-permute-start | bytes 1327112 | tf_op jit(solution)/shard_map/ppermute | solution.py:16
  59.4 14.0 %collective-permute-start.8 = (bf16[128,1536]{1,0:T(8,128)(2,1)}, bf16[128,1536]{1,0:T(8,128)(2,1)S(1)}, u32[]{:S(2)}, u32[]{:S(2)}) collective-permute-start(bf16[128,1536]{1,0:T(8,128)(2,1)} %get-tuple-element.68), channel_id=1, source_target_pairs={{0,1},{1,2},{2,3},{3,0},{4,5},{5,6},{6,7},{7,4},{8,9},{9,10},{10,1... | collective-permute-start | bytes 1179656 | tf_op jit(solution)/shard_map/ppermute | solution.py:26
  62.1 19.1 %collective-permute-start.9 = (bf16[128,1536]{1,0:T(8,128)(2,1)}, bf16[128,1536]{1,0:T(8,128)(2,1)S(1)}, u32[]{:S(2)}, u32[]{:S(2)}) collective-permute-start(bf16[128,1536]{1,0:T(8,128)(2,1)} %get-tuple-element.68), channel_id=1, source_target_pairs={{0,3},{1,0},{2,1},{3,2},{4,7},{5,4},{6,5},{7,6},{8,11},{9,8},{10,9... | collective-permute-start | bytes 1179656 | tf_op jit(solution)/shard_map/ppermute | solution.py:26
  63.3 19.9 %collective-permute-start.11 = (bf16[128,1536]{1,0:T(8,128)(2,1)S(1)}, bf16[128,1536]{1,0:T(8,128)(2,1)S(1)}, u32[]{:S(2)}, u32[]{:S(2)}) collective-permute-start(bf16[128,1536]{1,0:T(8,128)(2,1)S(1)} %copy-done.24), channel_id=1, source_target_pairs={{0,8},{4,12},{8,0},{12,4},{16,24},{20,28},{24,16},{28,20},{1,9},{5... | collective-permute-start | bytes 1179656 | tf_op jit(solution)/shard_map/ppermute | solution.py:16
  63.7 20.0 %collective-permute-start.12 = (bf16[128,1536]{1,0:T(8,128)(2,1)S(1)}, bf16[128,1536]{1,0:T(8,128)(2,1)S(1)}, u32[]{:S(2)}, u32[]{:S(2)}) collective-permute-start(bf16[128,1536]{1,0:T(8,128)(2,1)S(1)} %copy-done.24), channel_id=1, source_target_pairs={{0,16},{4,20},{8,24},{12,28},{16,0},{20,4},{24,8},{28,12},{1,17},{... | collective-permute-start | bytes 1179656 | tf_op jit(solution)/shard_map/ppermute | solution.py:16
  64.4 21.1 %collective-permute-start.13 = (bf16[128,1536]{1,0:T(8,128)(2,1)S(1)}, bf16[128,1536]{1,0:T(8,128)(2,1)S(1)}, u32[]{:S(2)}, u32[]{:S(2)}) collective-permute-start(bf16[128,1536]{1,0:T(8,128)(2,1)S(1)} %copy-done.24), channel_id=1, source_target_pairs={{0,24},{4,28},{8,16},{12,20},{16,8},{20,12},{24,0},{28,4},{1,25},{... | collective-permute-start | bytes 1179656 | tf_op jit(solution)/shard_map/ppermute | solution.py:16
  73.4 12.6 %collective-permute-start.14 = (bf16[128,1536]{1,0:T(8,128)(2,1)S(1)}, bf16[128,1536]{1,0:T(8,128)(2,1)S(1)}, u32[]{:S(2)}, u32[]{:S(2)}) collective-permute-start(bf16[128,1536]{1,0:T(8,128)(2,1)S(1)} %copy-done.24), channel_id=1, source_target_pairs={{0,4},{4,0},{8,12},{12,8},{16,20},{20,16},{24,28},{28,24},{1,5},{5... | collective-permute-start | bytes 1179656 | tf_op jit(solution)/shard_map/ppermute | solution.py:16
  81.2 11.3 %collective-permute-start.10 = (bf16[128,1536]{1,0:T(8,128)(2,1)S(1)}, bf16[128,1536]{1,0:T(8,128)(2,1)S(1)}, u32[]{:S(2)}, u32[]{:S(2)}) collective-permute-start(bf16[128,1536]{1,0:T(8,128)(2,1)S(1)} %select_select_fusion), channel_id=1, source_target_pairs={{0,2},{3,1},{2,3},{1,0},{4,6},{7,5},{6,7},{5,4},{8,10},{11,9},{10,... | collective-permute-start | bytes 1179656 | tf_op jit(solution)/shard_map/ppermute | solution.py:334
  129.4 14.0 %collective-permute-start.22 = (bf16[128,1536]{1,0:T(8,128)(2,1)}, bf16[128,1536]{1,0:T(8,128)(2,1)S(1)}, u32[]{:S(2)}, u32[]{:S(2)}) collective-permute-start(bf16[128,1536]{1,0:T(8,128)(2,1)} %get-tuple-element.135), channel_id=1, source_target_pairs={{0,1},{1,2},{2,3},{3,0},{4,5},{5,6},{6,7},{7,4},{8,9},{9,10},{10,1... | collective-permute-start | bytes 1179656 | tf_op jit(solution)/shard_map/ppermute | solution.py:26
  130.5 19.7 %collective-permute-start.24 = (bf16[128,1536]{1,0:T(8,128)(2,1)S(1)}, bf16[128,1536]{1,0:T(8,128)(2,1)S(1)}, u32[]{:S(2)}, u32[]{:S(2)}) collective-permute-start(bf16[128,1536]{1,0:T(8,128)(2,1)S(1)} %get-tuple-element.136), channel_id=1, source_target_pairs={{0,3},{1,0},{2,1},{3,2},{4,7},{5,4},{6,5},{7,6},{8,11},{9,8},{10,9... | collective-permute-start | bytes 1179656 | tf_op jit(solution)/shard_map/ppermute | solution.py:26
  143.4 35.8 %collective-permute-start.28 = (bf16[1,2,192,1024]{3,2,1,0:T(8,128)(2,1)}, bf16[1,2,192,1024]{3,2,1,0:T(8,128)(2,1)}, u32[]{:S(2)}, u32[]{:S(2)}) collective-permute-start(bf16[1,2,192,1024]{3,2,1,0:T(8,128)(2,1)} %get-tuple-element.99), channel_id=1, source_target_pairs={{0,16},{4,20},{8,24},{12,28},{16,0},{20,4},{24,8},{28,12},{1,17},{... | collective-permute-start | bytes 2359304 | tf_op jit(solution)/shard_map/ppermute | solution.py:16
  143.9 35.3 %collective-permute-start.27 = (bf16[2,1,192,1024]{3,2,0,1:T(8,128)(2,1)}, bf16[2,1,192,1024]{3,2,0,1:T(8,128)(2,1)}, u32[]{:S(2)}, u32[]{:S(2)}) collective-permute-start(bf16[2,1,192,1024]{3,2,0,1:T(8,128)(2,1)} %bitcast.93), channel_id=1, source_target_pairs={{0,8},{4,12},{8,0},{12,4},{16,24},{20,28},{24,16},{28,20},{1,9},{5... | collective-permute-start | bytes 2359304 | tf_op jit(solution)/shard_map/ppermute | solution.py:16
  151.3 16.4 %all-to-all-start.1 = ((bf16[8,192,128]{2,1,0:T(8,128)(2,1)}), bf16[8,192,128]{2,1,0:T(8,128)(2,1)S(1)}, u32[]{:S(2)}, u32[]{:S(2)}) async-start(bf16[8,192,128]{2,1,0:T(8,128)(2,1)} %bitcast.91), calls=%async_computation.1 | async-start | bytes 786432 | tf_op jit(solution)/shard_map/all_to_all | solution.py:709
  170.1 11.2 %collective-permute-start.26 = (bf16[40,768]{1,0:T(8,128)(2,1)S(1)}, bf16[40,768]{1,0:T(8,128)(2,1)S(1)}, u32[]{:S(2)}, u32[]{:S(2)}) collective-permute-start(bf16[40,768]{1,0:T(8,128)(2,1)S(1)} %add_convert_fusion.1), channel_id=1, source_target_pairs={{0,8},{4,12},{8,0},{12,4},{16,24},{20,28},{24,16},{28,20},{1,9},{5... | collective-permute-start | bytes 184328 | tf_op jit(solution)/shard_map/ppermute | solution.py:16
  182.3 14.0 %collective-permute-start.33 = (bf16[192,384]{1,0:T(8,128)(2,1)S(1)}, bf16[192,384]{1,0:T(8,128)(2,1)S(1)}, u32[]{:S(2)}, u32[]{:S(2)}) collective-permute-start(bf16[192,384]{1,0:T(8,128)(2,1)S(1)} %copy-done.45), channel_id=1, source_target_pairs={{0,2},{1,3},{2,0},{3,1},{4,6},{5,7},{6,4},{7,5},{8,10},{9,11},{10,... | collective-permute-start | bytes 442376 | tf_op jit(solution)/shard_map/ppermute | solution.py:21
  184.4 11.9 %collective-permute-start.34 = (bf16[192,384]{1,0:T(8,128)(2,1)S(1)}, bf16[192,384]{1,0:T(8,128)(2,1)S(1)}, u32[]{:S(2)}, u32[]{:S(2)}) collective-permute-start(bf16[192,384]{1,0:T(8,128)(2,1)S(1)} %copy-done.44), channel_id=1, source_target_pairs={{0,3},{1,2},{2,1},{3,0},{4,7},{5,6},{6,5},{7,4},{8,11},{9,10},{10,... | collective-permute-start | bytes 442376 | tf_op jit(solution)/shard_map/ppermute | solution.py:21
  185.9 13.3 %collective-permute-start.36 = (bf16[1,1,192,1024]{3,2,1,0:T(8,128)(2,1)S(1)}, bf16[1,1,192,1024]{3,2,1,0:T(8,128)(2,1)S(1)}, u32[]{:S(2)}, u32[]{:S(2)}) collective-permute-start(bf16[1,1,192,1024]{3,2,1,0:T(8,128)(2,1)S(1)} %get-tuple-element.116), channel_id=1, source_target_pairs={{0,8},{4,12},{8,0},{12,4},{16,24},{20,28},{24,16},{28,20},{1,9},{5... | collective-permute-start | bytes 1179656 | tf_op jit(solution)/shard_map/ppermute | solution.py:16
  186.4 12.8 %collective-permute-start.35 = (bf16[1,1,192,1024]{3,2,1,0:T(8,128)(2,1)S(1)}, bf16[1,1,192,1024]{3,2,1,0:T(8,128)(2,1)S(1)}, u32[]{:S(2)}, u32[]{:S(2)}) collective-permute-start(bf16[1,1,192,1024]{3,2,1,0:T(8,128)(2,1)S(1)} %get-tuple-element.113), channel_id=1, source_target_pairs={{0,16},{4,20},{8,24},{12,28},{16,0},{20,4},{24,8},{28,12},{1,17},{... | collective-permute-start | bytes 1179656 | tf_op jit(solution)/shard_map/ppermute | solution.py:16
  (67 other events, 473.9 us)
